TPU v7x, 256 devices: a whole 4x4x8 slice. The times are simulated.
256 devices in a mesh: phase: 16 (over y_hi, x, core), chan: 16 (over z, y_lo).
Axes of the slice: x: 4, y: 4 (y_hi: 2, y_lo: 2; y = y_hi * 2 + y_lo), z: 8, core: 2. Of those that a mesh axis runs over, the one named last changes fastest.
Arguments:
- frames: bfloat16 [64, 32, 2048], P(None, 'phase', 'chan'), may hold values from -6 to 6
- temporal_taps: float32 [4, 3, 64], replicated, may hold values from -3 to 3
- conv_weights: bfloat16 [4, 64, 27, 2, 64], P(None, None, None, None, 'chan'), may hold values from -0.15625 to 0.15625
- cotangent: bfloat16 [64, 32, 2048], P(None, 'phase', 'chan'), may hold values from -16 to 16
Outputs:
- final_frames: bfloat16 [64, 32, 2048], P(None, 'phase', 'chan')
- grad_frames: bfloat16 [64, 32, 2048], P(None, 'phase', 'chan')
- grad_taps: float32 [4, 3, 64], replicated
- grad_weights: float32 [4, 64, 27, 2, 64], P(None, None, None, None, 'chan')
All inputs are finite; a program needn't handle non-finite values.
Results may differ from a plain program's by a relative error of at most 0.025.
Values may be sent and summed in bfloat16 or wider, within the bound.
No kernel may reach another device: no remote copies, remote signals or barrier semaphores. Data moves between devices by JAX's collectives and lax.ppermute only.
A program may use at most 64 MiB of HBM per device.

v0:
```python
import jax
import jax.numpy as jnp
from jax import lax
from jax.sharding import PartitionSpec as P

BLOCKS = 4
SY = 8
SZ = 16


cell_offsets = [
    (kernel_pos // 9 - 1, kernel_pos // 3 % 3 - 1, kernel_pos % 3 - 1) for kernel_pos in range(27)
]


def shifted(block, axis, distance):
    devices = range(lax.axis_size(axis))
    route = [((i - distance) % len(devices), i) for i in devices]
    return lax.ppermute(block, axis, route)


def padded_2(cells, sides, width):
    for axis, dim in sides:
        count = lax.axis_size(axis)
        ends = count - 1
        head = lax.slice_in_dim(cells, 0, width, axis=dim)
        tail = lax.slice_in_dim(cells, cells.shape[dim] - width, cells.shape[dim], axis=dim)
        cells = jnp.concatenate(
            [
                lax.ppermute(tail, axis, [(i, (i + 1) % count) for i in range(ends)]),
                cells,
                lax.ppermute(head, axis, [((i + 1) % count, i) for i in range(ends)]),
            ],
            axis=dim,
        )
    return cells


def within_plane(source, step_y, step_z):
    cell_count = source.shape[-1]
    last_dim = source.ndim - 1
    margin = SZ + 1
    moved = step_y * SZ + step_z
    padded = jnp.pad(source, [(0, 0)] * last_dim + [(margin, margin)])
    window = lax.slice_in_dim(padded, margin + moved, margin + moved + cell_count, axis=last_dim)
    places = jnp.arange(cell_count, dtype=jnp.int32)
    coord_y = places // SZ + step_y
    coord_z = places % SZ + step_z
    inside = (coord_y >= 0) & (coord_y < SY) & (coord_z >= 0) & (coord_z < SZ)
    return jnp.where(inside, window, jnp.zeros_like(window))


def shifted_cells(rimmed, step_x, step_y, step_z):
    planes = rimmed.shape[-2] - 2
    rows = lax.slice_in_dim(rimmed, 1 + step_x, 1 + step_x + planes, axis=rimmed.ndim - 2)
    moved = within_plane(rows, step_y, step_z)
    return moved.reshape(moved.shape[:-2] + (planes * moved.shape[-1],))


def offset_stack(rimmed, first, count, sign):
    picked = cell_offsets[first : first + count]
    return jnp.stack(
        [
            shifted_cells(rimmed, sign * offset[0], sign * offset[1], sign * offset[2])
            for offset in picked
        ],
        axis=1,
    )


def back_block(source, hops):
    if hops == 0:
        return source
    return shifted(source, "phase", hops)


def next_block(source, hops):
    if hops == 0:
        return source
    return shifted(source, "phase", -hops)


def neighbours(source, reach):
    phase_rows = source.shape[1]
    hops, rest = divmod(reach, phase_rows)
    if rest == 0:
        return (back_block(source, hops), next_block(source, hops))
    joined = jnp.concatenate([back_block(source, hops + 1), back_block(source, hops)], axis=1)
    behind = joined[:, phase_rows - rest : 2 * phase_rows - rest]
    joined = jnp.concatenate([next_block(source, hops), next_block(source, hops + 1)], axis=1)
    ahead = joined[:, rest : rest + phase_rows]
    return (behind, ahead)


def per_device(frames, temporal_taps, conv_weights, cotangent):
    chans, phase_rows, cell_count = frames.shape
    plane_cells = SY * SZ
    planes = cell_count // plane_cells
    state = frames
    saved = []
    for block_num in range(BLOCKS):
        reach = 2**block_num
        behind, ahead = neighbours(state, reach)
        tap_rows = temporal_taps[block_num][:, :, None, None]
        mixed = (
            tap_rows[0] * behind.astype(jnp.float32)
            + tap_rows[1] * state.astype(jnp.float32)
            + tap_rows[2] * ahead.astype(jnp.float32)
        ).astype(jnp.bfloat16)
        rimmed = padded_2(mixed.reshape(chans, phase_rows, planes, plane_cells), (("chan", 2),), 1)
        kernel = lax.all_gather(conv_weights[block_num], "chan", axis=3, tiled=True)
        conv_out = jnp.zeros((chans, 2, phase_rows, cell_count), jnp.float32)
        for first in range(0, 27, 9):
            group = offset_stack(rimmed, first, 9, 1)
            conv_out = conv_out + jnp.einsum(
                "ikpv,ikgo->ogpv",
                group,
                kernel[:, first : first + 9],
                preferred_element_type=jnp.float32,
            )
        value_part = conv_out[:, 0]
        gate_sig = jax.nn.sigmoid(conv_out[:, 1])
        saved.append((state, behind, ahead, rimmed, kernel, value_part, gate_sig))
        state = (state.astype(jnp.float32) + value_part * gate_sig).astype(jnp.bfloat16)
    grad_state = cotangent
    weight_grads = [None] * BLOCKS
    tap_grads = [None] * BLOCKS
    for block_num in reversed(range(BLOCKS)):
        reach = 2**block_num
        prior, behind, ahead, rimmed, kernel, value_part, gate_sig = saved[block_num]
        tap_rows = temporal_taps[block_num][:, :, None, None]
        grad_y = grad_state.astype(jnp.float32)
        grad_z = jnp.stack(
            [grad_y * gate_sig, grad_y * value_part * gate_sig * (1.0 - gate_sig)], axis=1
        ).astype(jnp.bfloat16)
        rim_grad = padded_2(
            grad_z.reshape(chans, 2, phase_rows, planes, plane_cells), (("chan", 3),), 1
        )
        grad_mix = jnp.zeros((chans, phase_rows, cell_count), jnp.float32)
        for first in range(0, 27, 3):
            group = offset_stack(rim_grad, first, 3, -1)
            grad_mix = grad_mix + jnp.einsum(
                "okgpv,ikgo->ipv",
                group,
                kernel[:, first : first + 3],
                preferred_element_type=jnp.float32,
            )
        kernel_parts = []
        for first in range(0, 27, 9):
            group = offset_stack(rimmed, first, 9, 1)
            kernel_parts.append(
                jnp.einsum("ikpv,ogpv->ikgo", group, grad_z, preferred_element_type=jnp.float32)
            )
        grad_kernel = jnp.concatenate(kernel_parts, axis=1)
        grad_tap = jnp.stack(
            [
                jnp.sum(grad_mix * behind.astype(jnp.float32), axis=(1, 2)),
                jnp.sum(grad_mix * prior.astype(jnp.float32), axis=(1, 2)),
                jnp.sum(grad_mix * ahead.astype(jnp.float32), axis=(1, 2)),
            ]
        )
        grad_low = grad_mix.astype(jnp.bfloat16)
        back_mix, ahead_mix = neighbours(grad_low, reach)
        grad_state = (
            grad_y
            + tap_rows[0] * ahead_mix.astype(jnp.float32)
            + tap_rows[1] * grad_low.astype(jnp.float32)
            + tap_rows[2] * back_mix.astype(jnp.float32)
        ).astype(jnp.bfloat16)
        kernel_piece = lax.psum_scatter(
            grad_kernel.astype(jnp.bfloat16), "chan", scatter_dimension=3, tiled=True
        )
        grad_kernel = lax.psum(kernel_piece, "phase").astype(jnp.float32)
        weight_grads[block_num] = grad_kernel
        tap_grads[block_num] = grad_tap
    grad_weights = jnp.stack(weight_grads)
    grad_taps = lax.psum(jnp.stack(tap_grads), ("phase", "chan"))
    return (state, grad_state, grad_taps, grad_weights)


def solution(mesh):
    in_specs = (
        P(None, "phase", "chan"),
        P(),
        P(None, None, None, None, "chan"),
        P(None, "phase", "chan"),
    )
    out_specs = (
        P(None, "phase", "chan"),
        P(None, "phase", "chan"),
        P(),
        P(None, None, None, None, "chan"),
    )
    return jax.shard_map(
        per_device, mesh=mesh, in_specs=in_specs, out_specs=out_specs, check_vma=False
    )
```

profile of v0, /device:TPU:7, one launch (start us, length us, event | category | flops | bytes accessed | tf_op | source)
XLA Modules:
  0.0 648.9 jit_solution(4640616665763876973)
XLA Ops:
  8.0 3.4 collective-permute-start
  12.5 34.2 %all-gather = bf16[1,64,27,2,64]{1,3,2,0,4:T(2,128)(2,1)S(1)} all-gather(bf16[1,64,27,2,4]{1,3,2,0,4:T(2,128)(2,1)S(1)} %copy.558), channel_id=2, replica_groups=mesh['phase'=16,'chan'=16] {'chan'}, dimensions={4}, use_global_device_ids=true | all-gather | bytes 470016 | tf_op jit(solution)/shard_map/all_gather | solution.py:111
  49.0 4.0 collective-permute-start.2
  56.6 13.0 %collective-permute-start.4 = (bf16[64,2,128]{2,0,1:T(8,128)(2,1)S(1)}, bf16[64,2,128]{2,0,1:T(8,128)(2,1)S(1)}, u32[]{:S(2)}, u32[]{:S(2)}) collective-permute-start(bf16[64,2,128]{2,0,1:T(8,128)(2,1)S(1)} %fusion.164), channel_id=1, source_target_pairs={{240,0},{0,16},{16,32},{32,48},{48,64},{64,80},{80,96},{96,112},{1... | collective-permute-start | bytes 98312 | tf_op jit(solution)/shard_map/ppermute | solution.py:19
  70.7 5.9 collective-permute-done.5
  77.2 2.9 collective-permute-start.6
  81.4 31.7 %all-gather.1 = bf16[1,64,27,2,64]{1,3,2,0,4:T(2,128)(2,1)S(1)} all-gather(bf16[1,64,27,2,4]{1,3,2,0,4:T(2,128)(2,1)S(1)} %copy.559), channel_id=3, replica_groups=mesh['phase'=16,'chan'=16] {'chan'}, dimensions={4}, use_global_device_ids=true | all-gather | bytes 470016 | tf_op jit(solution)/shard_map/all_gather | solution.py:111
  118.6 3.7 collective-permute-done.9
  122.9 2.8 collective-permute-start.10
  127.0 33.8 %all-gather.2 = bf16[1,64,27,2,64]{1,3,2,0,4:T(2,128)(2,1)S(1)} all-gather(bf16[1,64,27,2,4]{1,3,2,0,4:T(2,128)(2,1)S(1)} %copy.560), channel_id=4, replica_groups=mesh['phase'=16,'chan'=16] {'chan'}, dimensions={4}, use_global_device_ids=true | all-gather | bytes 470016 | tf_op jit(solution)/shard_map/all_gather | solution.py:111
  163.5 3.0 collective-permute-start.13
  167.7 2.5 collective-permute-done.13
  174.4 30.8 %all-gather.3 = bf16[1,64,27,2,64]{1,3,2,0,4:T(2,128)(2,1)S(1)} all-gather(bf16[1,64,27,2,4]{1,3,2,0,4:T(2,128)(2,1)S(1)} %copy.561), channel_id=5, replica_groups=mesh['phase'=16,'chan'=16] {'chan'}, dimensions={4}, use_global_device_ids=true | all-gather | bytes 470016 | tf_op jit(solution)/shard_map/all_gather | solution.py:111
  214.5 4.0 collective-permute-start.17
  228.9 3.1 collective-permute-done.18
  236.0 4.0 collective-permute-start.21
  247.8 4.1 collective-permute-done.22
  253.8 4.6 collective-permute-start.25
  264.3 26.8 %collective-permute-start.27 = (bf16[64,2,128]{2,0,1:T(8,128)(2,1)S(1)}, bf16[64,2,128]{2,0,1:T(8,128)(2,1)S(1)}, u32[]{:S(2)}, u32[]{:S(2)}) collective-permute-start(bf16[64,2,128]{2,0,1:T(8,128)(2,1)S(1)} %get-tuple-element.46), channel_id=1, source_target_pairs={{240,0},{0,16},{16,32},{32,48},{48,64},{64,80},{80,96},{96,112},{1... | collective-permute-start | bytes 98312 | tf_op jit(solution)/shard_map/ppermute | solution.py:19
  292.1 5.9 collective-permute-done.26
  299.9 4.9 collective-permute-start.29
  313.8 85.8 %psum.35 = f32[4,3,64]{2,1,0:T(4,128)S(1)} all-reduce(f32[4,3,64]{2,1,0:T(4,128)S(1)} %pad_maximum_fusion.48), channel_id=1, replica_groups=mesh['phase'=16,'chan'=16] {'phase','chan'}, use_global_device_ids=true, to_apply=%region_12.13 | all-reduce | flops 768 | bytes 6144 | tf_op jit(solution)/shard_map/psum | solution.py:177
  400.2 91.4 %all-reduce.33.cloned.1.call-done = (bf16[64,27,2,64]{0,3,1,2:T(8,128)(2,1)}, bf16[64,27,2,64]{0,3,1,2:T(8,128)(2,1)}, bf16[64,27,2,64]{0,3,1,2:T(8,128)(2,1)}, bf16[64,27,2,64]{0,3,1,2:T(8,128)(2,1)}) async-done(((bf16[64,27,2,64]{0,3,1,2:T(8,128)(2,1)}, bf16[64,27,2,64]{0,3,1,2:T(8,128)(2,1)}, bf16[64,27,2,64]{0,3,1,2:T(8,128)(2,1)}, bf16[64,27,2,64]{0,3,1,2:T(8,128)(2,1)}), ...) | async-done | bytes 1769488
  499.2 140.9 %all-reduce.35.cloned.1.call-done = (bf16[1,64,27,2,4]{1,4,2,3,0:T(4,128)(2,1)}, bf16[1,64,27,2,4]{1,4,2,3,0:T(4,128)(2,1)}, bf16[1,64,27,2,4]{1,4,2,3,0:T(4,128)(2,1)}, bf16[1,64,27,2,4]{1,4,2,3,0:T(4,128)(2,1)}) async-done(((bf16[1,64,27,2,4]{1,4,2,3,0:T(4,128)(2,1)}, bf16[1,64,27,2,4]{1,4,2,3,0:T(4,128)(2,1)}, bf16[1,64,27,2,4]{1,4,2,3,0:T(4,128)(2,1)}, bf16[1,64,27,2,4]{1,4,2,3,0:T(4,128)(2,1)}), ...) | async-done | bytes 110608 | tf_op jit(solution)/shard_map/psum | solution.py:173
  (397 shorter events, 85.1 us)
Async XLA Ops:
  7.2 484.4 %all-reduce.33.cloned.1.call-start = ((), (), s32[]{:S(2)}) async-start(), calls=%async_computation | async-start | bytes 7077888
  8.0 38.9 %collective-permute-start = (bf16[64,2,128]{2,0,1:T(8,128)(2,1)S(1)}, bf16[64,2,128]{2,0,1:T(8,128)(2,1)S(1)}, u32[]{:S(2)}, u32[]{:S(2)}) collective-permute-start(bf16[64,2,128]{2,0,1:T(8,128)(2,1)S(1)} %copy.143), channel_id=1, source_target_pairs={{240,0},{0,16},{16,32},{32,48},{48,64},{64,80},{80,96},{96,112},{1... | collective-permute-start | bytes 98312 | tf_op jit(solution)/shard_map/ppermute | solution.py:19
  11.4 35.5 %collective-permute-start.1 = (bf16[64,2,128]{2,0,1:T(8,128)(2,1)S(1)}, bf16[64,2,128]{2,0,1:T(8,128)(2,1)S(1)}, u32[]{:S(2)}, u32[]{:S(2)}) collective-permute-start(bf16[64,2,128]{2,0,1:T(8,128)(2,1)S(1)} %copy.143), channel_id=1, source_target_pairs={{16,0},{32,16},{48,32},{64,48},{80,64},{96,80},{112,96},{128,112},... | collective-permute-start | bytes 98312 | tf_op jit(solution)/shard_map/ppermute | solution.py:19
  56.6 14.1 %collective-permute-start.4 = (bf16[64,2,128]{2,0,1:T(8,128)(2,1)S(1)}, bf16[64,2,128]{2,0,1:T(8,128)(2,1)S(1)}, u32[]{:S(2)}, u32[]{:S(2)}) collective-permute-start(bf16[64,2,128]{2,0,1:T(8,128)(2,1)S(1)} %fusion.164), channel_id=1, source_target_pairs={{240,0},{0,16},{16,32},{32,48},{48,64},{64,80},{80,96},{96,112},{1... | collective-permute-start | bytes 98312 | tf_op jit(solution)/shard_map/ppermute | solution.py:19
  69.7 7.0 %collective-permute-start.5 = (bf16[64,2,128]{2,0,1:T(8,128)(2,1)S(1)}, bf16[64,2,128]{2,0,1:T(8,128)(2,1)S(1)}, u32[]{:S(2)}, u32[]{:S(2)}) collective-permute-start(bf16[64,2,128]{2,0,1:T(8,128)(2,1)S(1)} %fusion.164), channel_id=1, source_target_pairs={{16,0},{32,16},{48,32},{64,48},{80,64},{96,80},{112,96},{128,112},... | collective-permute-start | bytes 98312 | tf_op jit(solution)/shard_map/ppermute | solution.py:19
  77.2 36.1 %collective-permute-start.6 = (bf16[64,2,1,128]{3,0,1,2:T(8,128)(2,1)S(1)}, bf16[64,2,1,128]{3,0,1,2:T(8,128)(2,1)S(1)}, u32[]{:S(2)}, u32[]{:S(2)}) collective-permute-start(bf16[64,2,1,128]{3,0,1,2:T(8,128)(2,1)S(1)} %bitcast.1583), channel_id=1, source_target_pairs={{0,1},{1,2},{2,3},{3,4},{4,5},{5,6},{6,7},{7,8},{8,9},{9,10},{10,1... | collective-permute-start | bytes 98312 | tf_op jit(solution)/shard_map/ppermute | solution.py:30
  80.1 33.2 %collective-permute-start.7 = (bf16[64,2,1,128]{3,0,1,2:T(8,128)(2,1)S(1)}, bf16[64,2,1,128]{3,0,1,2:T(8,128)(2,1)S(1)}, u32[]{:S(2)}, u32[]{:S(2)}) collective-permute-start(bf16[64,2,1,128]{3,0,1,2:T(8,128)(2,1)S(1)} %bitcast.1584), channel_id=1, source_target_pairs={{1,0},{2,1},{3,2},{4,3},{5,4},{6,5},{7,6},{8,7},{9,8},{10,9},{11,1... | collective-permute-start | bytes 98312 | tf_op jit(solution)/shard_map/ppermute | solution.py:32
  122.9 38.1 %collective-permute-start.10 = (bf16[64,2,1,128]{3,0,1,2:T(8,128)(2,1)S(1)}, bf16[64,2,1,128]{3,0,1,2:T(8,128)(2,1)S(1)}, u32[]{:S(2)}, u32[]{:S(2)}) collective-permute-start(bf16[64,2,1,128]{3,0,1,2:T(8,128)(2,1)S(1)} %bitcast.1593), channel_id=1, source_target_pairs={{0,1},{1,2},{2,3},{3,4},{4,5},{5,6},{6,7},{7,8},{8,9},{9,10},{10,1... | collective-permute-start | bytes 98312 | tf_op jit(solution)/shard_map/ppermute | solution.py:30
  125.7 35.3 %collective-permute-start.11 = (bf16[64,2,1,128]{3,0,1,2:T(8,128)(2,1)S(1)}, bf16[64,2,1,128]{3,0,1,2:T(8,128)(2,1)S(1)}, u32[]{:S(2)}, u32[]{:S(2)}) collective-permute-start(bf16[64,2,1,128]{3,0,1,2:T(8,128)(2,1)S(1)} %bitcast.1594), channel_id=1, source_target_pairs={{1,0},{2,1},{3,2},{4,3},{5,4},{6,5},{7,6},{8,7},{9,8},{10,9},{11,1... | collective-permute-start | bytes 98312 | tf_op jit(solution)/shard_map/ppermute | solution.py:32
  163.5 6.8 %collective-permute-start.13 = (bf16[64,2,128]{2,0,1:T(8,128)(2,1)S(1)}, bf16[64,2,128]{2,0,1:T(8,128)(2,1)S(1)}, u32[]{:S(2)}, u32[]{:S(2)}) collective-permute-start(bf16[64,2,128]{2,0,1:T(8,128)(2,1)S(1)} %fusion.168), channel_id=1, source_target_pairs={{64,0},{80,16},{96,32},{112,48},{128,64},{144,80},{160,96},{176,11... | collective-permute-start | bytes 98312 | tf_op jit(solution)/shard_map/ppermute | solution.py:19
  170.8 36.5 %collective-permute-start.14 = (bf16[64,2,1,128]{3,0,1,2:T(8,128)(2,1)S(1)}, bf16[64,2,1,128]{3,0,1,2:T(8,128)(2,1)S(1)}, u32[]{:S(2)}, u32[]{:S(2)}) collective-permute-start(bf16[64,2,1,128]{3,0,1,2:T(8,128)(2,1)S(1)} %bitcast.1573), channel_id=1, source_target_pairs={{0,1},{1,2},{2,3},{3,4},{4,5},{5,6},{6,7},{7,8},{8,9},{9,10},{10,1... | collective-permute-start | bytes 98312 | tf_op jit(solution)/shard_map/ppermute | solution.py:30
  173.1 34.3 %collective-permute-start.15 = (bf16[64,2,1,128]{3,0,1,2:T(8,128)(2,1)S(1)}, bf16[64,2,1,128]{3,0,1,2:T(8,128)(2,1)S(1)}, u32[]{:S(2)}, u32[]{:S(2)}) collective-permute-start(bf16[64,2,1,128]{3,0,1,2:T(8,128)(2,1)S(1)} %bitcast.1574), channel_id=1, source_target_pairs={{1,0},{2,1},{3,2},{4,3},{5,4},{6,5},{7,6},{8,7},{9,8},{10,9},{11,1... | collective-permute-start | bytes 98312 | tf_op jit(solution)/shard_map/ppermute | solution.py:32
  212.9 8.3 %collective-permute-start.16 = (bf16[64,2,2,1,128]{4,0,2,1,3:T(8,128)(2,1)S(1)}, bf16[64,2,2,1,128]{4,0,2,1,3:T(8,128)(2,1)S(1)}, u32[]{:S(2)}, u32[]{:S(2)}) collective-permute-start(bf16[64,2,2,1,128]{4,0,2,1,3:T(8,128)(2,1)S(1)} %pad_maximum_fusion.40), channel_id=1, source_target_pairs={{1,0},{2,1},{3,2},{4,3},{5,4},{6,5},{7,6},{8,7},{9,8},{10,9},{11,1... | collective-permute-start | bytes 196616 | tf_op jit(solution)/shard_map/ppermute | solution.py:32
  214.5 8.4 %collective-permute-start.17 = (bf16[64,2,2,1,128]{4,0,2,1,3:T(8,128)(2,1)S(1)}, bf16[64,2,2,1,128]{4,0,2,1,3:T(8,128)(2,1)S(1)}, u32[]{:S(2)}, u32[]{:S(2)}) collective-permute-start(bf16[64,2,2,1,128]{4,0,2,1,3:T(8,128)(2,1)S(1)} %pad_maximum_fusion.40), channel_id=1, source_target_pairs={{0,1},{1,2},{2,3},{3,4},{4,5},{5,6},{6,7},{7,8},{8,9},{9,10},{10,1... | collective-permute-start | bytes 196616 | tf_op jit(solution)/shard_map/ppermute | solution.py:30
  232.1 9.5 %collective-permute-start.20 = (bf16[64,2,2,1,128]{4,0,2,1,3:T(8,128)(2,1)S(1)}, bf16[64,2,2,1,128]{4,0,2,1,3:T(8,128)(2,1)S(1)}, u32[]{:S(2)}, u32[]{:S(2)}) collective-permute-start(bf16[64,2,2,1,128]{4,0,2,1,3:T(8,128)(2,1)S(1)} %get-tuple-element.110), channel_id=1, source_target_pairs={{1,0},{2,1},{3,2},{4,3},{5,4},{6,5},{7,6},{8,7},{9,8},{10,9},{11,1... | collective-permute-start | bytes 196616 | tf_op jit(solution)/shard_map/ppermute | solution.py:32
  252.2 9.0 %collective-permute-start.24 = (bf16[64,2,2,1,128]{4,0,2,1,3:T(8,128)(2,1)S(1)}, bf16[64,2,2,1,128]{4,0,2,1,3:T(8,128)(2,1)S(1)}, u32[]{:S(2)}, u32[]{:S(2)}) collective-permute-start(bf16[64,2,2,1,128]{4,0,2,1,3:T(8,128)(2,1)S(1)} %pad_maximum_fusion.42), channel_id=1, source_target_pairs={{1,0},{2,1},{3,2},{4,3},{5,4},{6,5},{7,6},{8,7},{9,8},{10,9},{11,1... | collective-permute-start | bytes 196616 | tf_op jit(solution)/shard_map/ppermute | solution.py:32
  253.8 8.9 %collective-permute-start.25 = (bf16[64,2,2,1,128]{4,0,2,1,3:T(8,128)(2,1)S(1)}, bf16[64,2,2,1,128]{4,0,2,1,3:T(8,128)(2,1)S(1)}, u32[]{:S(2)}, u32[]{:S(2)}) collective-permute-start(bf16[64,2,2,1,128]{4,0,2,1,3:T(8,128)(2,1)S(1)} %pad_maximum_fusion.42), channel_id=1, source_target_pairs={{0,1},{1,2},{2,3},{3,4},{4,5},{5,6},{6,7},{7,8},{8,9},{9,10},{10,1... | collective-permute-start | bytes 196616 | tf_op jit(solution)/shard_map/ppermute | solution.py:30
  264.3 27.8 %collective-permute-start.27 = (bf16[64,2,128]{2,0,1:T(8,128)(2,1)S(1)}, bf16[64,2,128]{2,0,1:T(8,128)(2,1)S(1)}, u32[]{:S(2)}, u32[]{:S(2)}) collective-permute-start(bf16[64,2,128]{2,0,1:T(8,128)(2,1)S(1)} %get-tuple-element.46), channel_id=1, source_target_pairs={{240,0},{0,16},{16,32},{32,48},{48,64},{64,80},{80,96},{96,112},{1... | collective-permute-start | bytes 98312 | tf_op jit(solution)/shard_map/ppermute | solution.py:19
  291.1 7.0 %collective-permute-start.26 = (bf16[64,2,128]{2,0,1:T(8,128)(2,1)S(1)}, bf16[64,2,128]{2,0,1:T(8,128)(2,1)S(1)}, u32[]{:S(2)}, u32[]{:S(2)}) collective-permute-start(bf16[64,2,128]{2,0,1:T(8,128)(2,1)S(1)} %get-tuple-element.46), channel_id=1, source_target_pairs={{16,0},{32,16},{48,32},{64,48},{80,64},{96,80},{112,96},{128,112},... | collective-permute-start | bytes 98312 | tf_op jit(solution)/shard_map/ppermute | solution.py:19
  298.2 10.1 %collective-permute-start.28 = (bf16[64,2,2,1,128]{4,0,2,1,3:T(8,128)(2,1)S(1)}, bf16[64,2,2,1,128]{4,0,2,1,3:T(8,128)(2,1)S(1)}, u32[]{:S(2)}, u32[]{:S(2)}) collective-permute-start(bf16[64,2,2,1,128]{4,0,2,1,3:T(8,128)(2,1)S(1)} %pad_maximum_fusion.43), channel_id=1, source_target_pairs={{1,0},{2,1},{3,2},{4,3},{5,4},{6,5},{7,6},{8,7},{9,8},{10,9},{11,1... | collective-permute-start | bytes 196616 | tf_op jit(solution)/shard_map/ppermute | solution.py:32
  299.9 10.6 %collective-permute-start.29 = (bf16[64,2,2,1,128]{4,0,2,1,3:T(8,128)(2,1)S(1)}, bf16[64,2,2,1,128]{4,0,2,1,3:T(8,128)(2,1)S(1)}, u32[]{:S(2)}, u32[]{:S(2)}) collective-permute-start(bf16[64,2,2,1,128]{4,0,2,1,3:T(8,128)(2,1)S(1)} %pad_maximum_fusion.43), channel_id=1, source_target_pairs={{0,1},{1,2},{2,3},{3,4},{4,5},{5,6},{6,7},{7,8},{8,9},{9,10},{10,1... | collective-permute-start | bytes 196616 | tf_op jit(solution)/shard_map/ppermute | solution.py:30
  308.3 331.8 %all-reduce.35.cloned.1.call-start = ((), (), s32[]{:S(2)}) async-start(), calls=%async_computation.1 | async-start | bytes 442368 | tf_op jit(solution)/shard_map/psum | solution.py:173
  312.1 185.7 %collective-permute-start.31 = (bf16[64,2,128]{2,0,1:T(8,128)(2,1)S(1)}, bf16[64,2,128]{2,0,1:T(8,128)(2,1)S(1)}, u32[]{:S(2)}, u32[]{:S(2)}) collective-permute-start(bf16[64,2,128]{2,0,1:T(8,128)(2,1)S(1)} %get-tuple-element.45), channel_id=1, source_target_pairs={{240,0},{0,16},{16,32},{32,48},{48,64},{64,80},{80,96},{96,112},{1... | collective-permute-start | bytes 98312 | tf_op jit(solution)/shard_map/ppermute | solution.py:19
  313.1 184.7 %collective-permute-start.30 = (bf16[64,2,128]{2,0,1:T(8,128)(2,1)S(1)}, bf16[64,2,128]{2,0,1:T(8,128)(2,1)S(1)}, u32[]{:S(2)}, u32[]{:S(2)}) collective-permute-start(bf16[64,2,128]{2,0,1:T(8,128)(2,1)S(1)} %get-tuple-element.45), channel_id=1, source_target_pairs={{16,0},{32,16},{48,32},{64,48},{80,64},{96,80},{112,96},{128,112},... | collective-permute-start | bytes 98312 | tf_op jit(solution)/shard_map/ppermute | solution.py:19
  (91 other events, 1605.3 us)
Sparse Core Ops, SparseCore 0:
  308.4 183.0 all-reduce.32
  497.9 142.1 all-reduce.34
where the time goes:
time: 651 us; the launch traced here: 649 us
  waiting for transfers between devices  264 us (41%)
  blocking collectives  216 us (33%)
  starting transfers between devices  93.6 us (14%)
  local copies, waits for them, and re-layouts  28.6 us (4%)
  between operations  16.5 us (3%)
  other arithmetic  15.3 us (2%)
  matrix products  14.9 us (2%)
    psum x1, waiting for transfers between devices, per_device(): grad_kernel = lax.psum(kernel_piece, 'phase').astype(jnp.float32)  141 us
    all_gather x4, blocking collectives, per_device(): kernel = lax.all_gather(conv_weights[block_num], 'chan', axis=3, tiled=True)  130 us
    unnamed x3, waiting for transfers between devices  91.4 us
    psum x1, blocking collectives, per_device(): grad_taps = lax.psum(jnp.stack(tap_grads), ('phase', 'chan'))  85.8 us
    ppermute x16, starting transfers between devices, shifted(): return lax.ppermute(block, axis, route)  53.4 us
    ppermute x16, waiting for transfers between devices, shifted(): return lax.ppermute(block, axis, route)  31.2 us
    ppermute x8, starting transfers between devices, padded_2(): lax.ppermute(tail, axis, [(i, (i + 1) % count) for i in range(ends)])  29.5 us
    unnamed x172, local copies, waits for them, and re-layouts  20.6 us
  transfers between devices with their start and end apart: 34, of which 15 were waited for; matrix products, arithmetic and copies ran while one was open for 4% of the time, Pallas kernels for 0%

commit v1 on v0

v1 whole, which is shorter than its diff:
```python
import functools

import jax
import jax.numpy as jnp
from jax import lax
from jax.experimental import pallas as pl
from jax.experimental.pallas import tpu as pltpu
from jax.sharding import PartitionSpec as P


BLOCKS = 4
SY = 8
SZ = 16
CELLS = SY * SZ
CHANS = 64
OFFSETS = 27
DEPTH = OFFSETS * CHANS
f32 = jnp.float32
bf16 = jnp.bfloat16


def call(body, out_shape, *args, scratch=(), flops=1_000_000, room=12):
    size = sum(a.size * a.dtype.itemsize for a in args)
    return pl.pallas_call(
        body,
        out_shape=out_shape,
        scratch_shapes=list(scratch),
        compiler_params=pltpu.CompilerParams(vmem_limit_bytes=room << 20),
        cost_estimate=pl.CostEstimate(flops=flops, bytes_accessed=size, transcendentals=0),
    )(*args)


def shaped(shape, kind):
    return jax.ShapeDtypeStruct(shape, kind)


def inside_masks(sign):
    places = lax.broadcasted_iota(jnp.int32, (1, CELLS), 1)
    masks = []
    for kk in range(9):
        dy, dz = sign * (kk // 3 - 1), sign * (kk % 3 - 1)
        y, z = places // SZ + dy, places % SZ + dz
        masks.append((y >= 0) & (y < SY) & (z >= 0) & (z < SZ))
    return masks


def spread_unit(unit, masks, sign):
    wide = unit.astype(f32)
    pieces = []
    for kk in range(9):
        step = sign * ((kk // 3 - 1) * SZ + kk % 3 - 1)
        if step == 0:
            pieces.append(unit)
        else:
            moved = pltpu.roll(wide, (-step) % CELLS, 1)
            pieces.append(jnp.where(masks[kk], moved, 0.0).astype(bf16))
    return pieces


def fill_columns(columns, planes, sign):
    masks = inside_masks(sign)
    rows = planes[0][0].shape[0]
    for dx in range(3):
        source = planes[dx] if sign > 0 else planes[2 - dx]
        for t, unit in enumerate(source):
            for kk, piece in enumerate(spread_unit(unit, masks, sign)):
                start = (dx * 9 + kk) * rows
                columns[start : start + rows, t * CELLS : (t + 1) * CELLS] = piece


def sort_matrix(transposed):
    r = lax.broadcasted_iota(jnp.int32, (128, 128), 0)
    c = lax.broadcasted_iota(jnp.int32, (128, 128), 1)
    if transposed:
        r, c = c, r
    wanted = (r % 64) // 4 * 8 + r // 64 * 4 + r % 4
    return jnp.where(c == wanted, 1.0, 0.0).astype(bf16)


def sort_kernel(raw, out):
    order = sort_matrix(False)
    for n in range(2):
        rows = raw[:, 8 * n : 8 * n + 8, :].reshape(128, DEPTH)
        out[n] = jnp.dot(order, rows, preferred_element_type=f32).astype(bf16)


def flip_kernel(weights, out):
    r = lax.broadcasted_iota(jnp.int32, (CHANS, CHANS), 0)
    c = lax.broadcasted_iota(jnp.int32, (CHANS, CHANS), 1)
    eye = jnp.where(r == c, 1.0, 0.0).astype(bf16)
    for n in range(2):
        for k in range(OFFSETS):
            piece = weights[n, :, k * CHANS : (k + 1) * CHANS]
            turned = lax.dot_general(
                eye, piece, (((1,), (1,)), ((), ())), preferred_element_type=f32
            )
            out[n, :, k * 128 : (k + 1) * 128] = turned.astype(bf16)


def tap_columns(taps, block):
    return [taps[:, 3 * block + n : 3 * block + n + 1] for n in range(3)]


def mix(t, before, now, after):
    total = t[0] * before.astype(f32) + t[1] * now.astype(f32) + t[2] * after.astype(f32)
    return total.astype(bf16)


def mix_kernel(block, taps, state, behind, ahead, out):
    t = tap_columns(taps, block)
    for n in range(2):
        out[n] = mix(t, behind[n], state[n], ahead[n])


def front_mix_kernel(taps, own, back1, next1, back2, next2, mixed, line):
    t = tap_columns(taps, 0)
    for x in range(5):
        f = [back2[x, 0], back1[x, 0], back1[x, 1], own[x, 0], own[x, 1]]
        f += [next1[x, 0], next1[x, 1], next2[x, 0]]
        for q in range(6):
            mixed[x, q] = mix(t, f[q], f[q + 1], f[q + 2])
        if x == 2:
            for q in range(4):
                line[q] = f[q + 2]


def gated_sum(conv, n):
    v = conv[:CHANS, n * CELLS : (n + 1) * CELLS]
    s = jax.nn.sigmoid(conv[CHANS:, n * CELLS : (n + 1) * CELLS])
    return v, s


def front_kernel(
    edge, taps, weights, mixed, own, back1, next1,
    value0, gate0, line1, mixed1, value1, gate1, after, columns, narrow,
):
    masks = inside_masks(1)
    for x in range(5):
        for q in range(6):
            for kk, piece in enumerate(spread_unit(mixed[x, q], masks, 1)):
                columns[x, kk * CHANS : (kk + 1) * CHANS, q * CELLS : (q + 1) * CELLS] = piece
    t = tap_columns(taps, 1)
    third = 9 * CHANS
    planes = []
    for x in range(3):
        conv = jnp.zeros((2 * CHANS, 6 * CELLS), f32)
        for dx in range(3):
            conv = conv + jnp.dot(
                weights[0, :, dx * third : (dx + 1) * third],
                columns[x + dx],
                preferred_element_type=f32,
            )
        f = [back1[x + 1, 0], back1[x + 1, 1], own[x + 1, 0], own[x + 1, 1]]
        f += [next1[x + 1, 0], next1[x + 1, 1]]
        states = []
        for q in range(6):
            v, s = gated_sum(conv, q)
            state = f[q].astype(f32) + v * s
            if x == 1:
                state = state.astype(bf16)
                line1[q] = state
                if q in (2, 3):
                    value0[q - 2] = v
                    gate0[q - 2] = s
            else:
                flag = edge[x // 2 : x // 2 + 1, :] > 0.5
                state = jnp.where(flag, state, 0.0).astype(bf16)
            states.append(state)
        units = [mix(t, states[n], states[n + 2], states[n + 4]) for n in range(2)]
        for n in range(2):
            mixed1[x, n] = units[n]
        planes.append(units)
    fill_columns(narrow, planes, 1)
    conv = jnp.dot(weights[1], narrow[...], preferred_element_type=f32)
    for n in range(2):
        v, s = gated_sum(conv, n)
        value1[n] = v
        gate1[n] = s
        after[n] = (line1[n + 2].astype(f32) + v * s).astype(bf16)


def conv_kernel(which, weights, mixed, left, right, state, *rest):
    fill_columns(rest[-1], [[a[0], a[1]] for a in (left, mixed, right)], 1)
    conv = jnp.dot(weights[which], rest[-1][...], preferred_element_type=f32)
    for n in range(2):
        v, s = gated_sum(conv, n)
        after = (state[n].astype(f32) + v * s).astype(bf16)
        if which == 0:
            rest[0][n] = v
            rest[1][n] = s
            rest[2][n] = after
        else:
            rest[1][n, :CHANS], rest[1][n, CHANS:] = gated(rest[0][n].astype(f32), v, s)
            rest[2][n] = after


def gated(y, v, s):
    return (y * s).astype(bf16), (y * v * s * (1.0 - s)).astype(bf16)


def whole_line(block, line):
    shift = min(2**block, 2)
    if len(line) == 1:
        units = [line[0][n] for n in range(2 + 2 * shift)]
    else:
        units = [ref[n] for ref in line for n in range(2)]
    return shift, units


def data_kernel(block, weight, gz, left, right, *rest):
    line, (low, tap, columns) = rest[:-3], rest[-3:]
    fill_columns(columns, [[a[0], a[1]] for a in (left, gz, right)], -1)
    grad = jnp.dot(weight[block % 2], columns[...], preferred_element_type=f32)
    shift, units = whole_line(block, line)
    totals = [0.0, 0.0, 0.0]
    for n in range(2):
        m = grad[:, n * CELLS : (n + 1) * CELLS]
        low[n] = m.astype(bf16)
        for which in range(3):
            totals[which] = totals[which] + m * units[n + which * shift].astype(f32)
    for which in range(3):
        tap[:, which : which + 1] = jnp.sum(totals[which], axis=1, keepdims=True)


def weight_kernel(offsets, gz, *rest):
    sources, (out, columns) = rest[:-2], rest[-2:]
    if len(sources) == 1:
        x, t = offsets
        planes = [[sources[0][x + n, t], sources[0][x + n, t + 1]] for n in range(3)]
    else:
        planes = [[a[0], a[1]] for a in sources]
    fill_columns(columns, planes, 1)
    both = jnp.concatenate([gz[0], gz[1]], axis=1)
    both = jnp.dot(sort_matrix(True), both, preferred_element_type=f32).astype(bf16)
    grad = lax.dot_general(
        columns[...], both, (((1,), (1,)), ((), ())), preferred_element_type=f32
    )
    out[:13] = grad[: 13 * 128].astype(bf16).reshape(13, 128, 128)
    out[13, :CHANS] = grad[13 * 128 :].astype(bf16)
    out[13, CHANS:] = jnp.zeros((CHANS, 128), bf16)
    out[14:] = jnp.zeros((2, 128, 128), bf16)


def turned_sum(pieces, start):
    total = pieces[0, start : start + 128].astype(f32)
    for n in range(1, 16):
        total = total + pieces[n, start : start + 128].astype(f32)
    r = lax.broadcasted_iota(jnp.int32, (128, 128), 0)
    c = lax.broadcasted_iota(jnp.int32, (128, 128), 1)
    eye = jnp.where(r == c, 1.0, 0.0).astype(bf16)
    swapped = lax.dot_general(
        eye, total.astype(bf16), (((1,), (1,)), ((), ())), preferred_element_type=f32
    )
    return swapped.astype(bf16)


def part_kernel(pieces, out):
    for n in range(3):
        out[2 - n] = turned_sum(pieces, 128 * n)


def halves(value):
    high = value.astype(bf16)
    low = (value - high.astype(f32)).astype(bf16)
    return high, low


def pack_kernel(pieces, later, taps, out):
    parts = [turned_sum(pieces, 0), later[0], later[1], later[2]]
    high, low = halves(taps[...])
    for j in range(16):
        for b in range(BLOCKS):
            out[j, 8 * b : 8 * b + 8] = parts[b][8 * j : 8 * j + 8]
        out[j, 32:40] = high
        out[j, 40:48] = low


def repack_kernel(pieces, out):
    total = pieces[0].astype(f32)
    for n in range(1, 16):
        total = total + pieces[n].astype(f32)
    high, low = halves(total[32:40] + total[40:48])
    grads = total[:32].astype(bf16)
    for p in range(16):
        out[p, :32] = grads
        out[p, 32:40] = high
        out[p, 40:48] = low


def back_state(block, taps, grad, low, behind, ahead):
    shift, units = whole_line(block, (behind, low, ahead)) if block else (1, None)
    if block == 0:
        units = [behind[0], low[0], low[1], ahead[0]]
    t = tap_columns(taps, block)
    return [
        (
            grad[n].astype(f32)
            + t[0] * units[n + 2 * shift].astype(f32)
            + t[1] * units[n + shift].astype(f32)
            + t[2] * units[n].astype(f32)
        ).astype(bf16)
        for n in range(2)
    ]


def last_kernel(block, taps, grad, low, behind, ahead, out):
    for n, g in enumerate(back_state(block, taps, grad, low, behind, ahead)):
        out[n] = g


def step_kernel(block, taps, grad, low, behind, ahead, value, gate, out, gz):
    for n, g in enumerate(back_state(block, taps, grad, low, behind, ahead)):
        out[n] = g
        a, b = gated(g.astype(f32), value[n], gate[n])
        gz[n, :CHANS] = a
        gz[n, CHANS:] = b


def beside(cells, axis, distance):
    count = lax.axis_size(axis)
    pairs = [(i, i + distance) for i in range(count) if 0 <= i + distance < count]
    return lax.ppermute(cells, axis, pairs)


def sides(cells, axis):
    return beside(cells, axis, 1), beside(cells, axis, -1)


def turned(block, distance):
    count = lax.axis_size("phase")
    return lax.ppermute(block, "phase", [((i - distance) % count, i) for i in range(count)])


def neighbours(source, reach):
    if reach == 1:
        return turned(source[1:], 1), turned(source[:1], -1)
    return turned(source, reach // 2), turned(source, -(reach // 2))


def spread(piece, axis):
    count = lax.axis_size(axis)
    copies = jnp.broadcast_to(piece[None], (count,) + piece.shape)
    return lax.all_to_all(copies, axis, 0, 0, tiled=True)


def per_device(frames, temporal_taps, conv_weights, cotangent):
    groups = lax.axis_size("chan")
    own = CHANS // groups
    rows = jnp.transpose(conv_weights, (0, 3, 4, 2, 1)).reshape(BLOCKS, 2 * own, DEPTH)
    taps = temporal_taps.reshape(3 * BLOCKS, CHANS).T
    unit = (2, CHANS, CELLS)
    gunit = (2, 2 * CHANS, CELLS)
    state = jnp.transpose(frames, (1, 0, 2))
    grad = jnp.transpose(cotangent, (1, 0, 2))
    columns = pltpu.VMEM((DEPTH, 2 * CELLS), bf16)
    wide_columns = pltpu.VMEM((2 * DEPTH, 2 * CELLS), bf16)
    place = lax.axis_index("chan")
    edge = jnp.stack([place > 0, place < groups - 1]).astype(f32)
    edge = jnp.broadcast_to(edge[:, None], (2, CELLS))

    raw = []
    for n in range(2):
        raw.append(spread(rows[2 * n : 2 * n + 2].reshape(4 * own, DEPTH), "chan"))
    weights = [call(sort_kernel, shaped((2, 128, DEPTH), bf16), r) for r in raw]

    cells = [beside(state, "chan", d) for d in (2, 1, -1, -2)]
    here = jnp.stack([cells[0], cells[1], state, cells[2], cells[3]])
    back1, next1 = turned(here, 1), turned(here, -1)
    back2, next2 = turned(here[:, 1:], 2), turned(here[:, :1], -2)
    mixed0, line0 = call(
      front_mix_kernel,
      [shaped((5, 6, CHANS, CELLS), bf16), shaped((4, CHANS, CELLS), bf16)],
      taps, here, back1, next1, back2, next2,
    )
    value0, gate0, line1, mixed1, value1, gate1, state = call(
        front_kernel,
        [
            shaped(unit, f32),
            shaped(unit, f32),
            shaped((6, CHANS, CELLS), bf16),
            shaped((3, 2, CHANS, CELLS), bf16),
            shaped(unit, f32),
            shaped(unit, f32),
            shaped(unit, bf16),
        ],
        edge, taps, weights[0], mixed0, here, back1, next1,
        scratch=[pltpu.VMEM((5, 9 * CHANS, 6 * CELLS), bf16), columns],
    )
    saved = [
        ((line0,), (mixed0,), (1, 2), value0, gate0),
        ((line1,), (mixed1,), (0, 0), value1, gate1),
    ]
    for b in range(2, BLOCKS):
        prior = state
        behind, ahead = neighbours(state, 2**b)
        mixed = call(
            functools.partial(mix_kernel, b), shaped(unit, bf16), taps, state, behind, ahead
        )
        left, right = sides(mixed, "chan")
        if b < BLOCKS - 1:
            value, gate, state = call(
                functools.partial(conv_kernel, 0),
                [shaped(unit, f32), shaped(unit, f32), shaped(unit, bf16)],
                weights[1], mixed, left, right, state,
                scratch=[columns],
            )
            saved.append(((behind, prior, ahead), (left, mixed, right), None, value, gate))
        else:
            gz, state = call(
                functools.partial(conv_kernel, 1),
                [shaped(gunit, bf16), shaped(unit, bf16)],
                weights[1], mixed, left, right, state, grad,
                scratch=[columns],
            )
            saved.append(((behind, prior, ahead), (left, mixed, right), None, None, None))
    final = state
    backs = [call(flip_kernel, shaped((2, CHANS, 2 * DEPTH), bf16), w) for w in weights]

    held = []
    tap_grads = [None] * BLOCKS
    for b in reversed(range(BLOCKS)):
        line, mixed, offsets, _, _ = saved[b]
        gleft, gright = sides(gz, "chan")
        pieces = call(
            functools.partial(weight_kernel, offsets),
            shaped((16, 128, 128), bf16),
            gz, *mixed,
            scratch=[columns],
        )
        held.append(pieces)
        if b == 1:
            early = jnp.concatenate(held, axis=1)
            early = lax.all_to_all(early, "phase", 0, 0, tiled=True)
        if b == 0:
            late = lax.all_to_all(pieces, "phase", 0, 0, tiled=True)
        low, tap_grads[b] = call(
            functools.partial(data_kernel, b),
            [shaped(unit, bf16), shaped((CHANS, 3), f32)],
            backs[b // 2], gz, gleft, gright, *line,
            scratch=[wide_columns],
        )
        behind, ahead = neighbours(low, 2**b)
        if b == 0:
            grad = call(
                functools.partial(last_kernel, b),
                shaped(unit, bf16),
                taps, grad, low, behind, ahead,
            )
        else:
            grad, gz = call(
                functools.partial(step_kernel, b),
                [shaped(unit, bf16), shaped(gunit, bf16)],
                taps, grad, low, behind, ahead, saved[b - 1][3], saved[b - 1][4],
            )
    parts = call(part_kernel, shaped((3, 128, 128), bf16), early)
    tap_rows = jnp.concatenate(tap_grads, axis=1).T.reshape(6, 2 * CHANS)
    tap_rows = jnp.pad(tap_rows, [(0, 2), (0, 0)])
    packed = call(pack_kernel, shaped((16, 48, 128), bf16), late, parts, tap_rows)
    packed = lax.all_to_all(packed, "chan", 0, 0, tiled=True)
    packed = call(repack_kernel, shaped((16, 48, 128), bf16), packed)
    packed = lax.all_to_all(packed, "phase", 0, 0, tiled=True)
    grad_rows = packed[:14, :32].astype(f32).reshape(14, BLOCKS, 2, own, 2, CHANS)
    grad_rows = jnp.transpose(grad_rows, (1, 5, 0, 4, 2, 3)).reshape(BLOCKS, CHANS, 28, 2, own)
    grad_weights = grad_rows[:, :, :OFFSETS]
    grad_taps = jnp.sum(packed[:, 32:].astype(f32), axis=0)
    grad_taps = (grad_taps[:6] + grad_taps[8:14]).reshape(BLOCKS, 3, CHANS)
    return (
        jnp.transpose(final, (1, 0, 2)),
        jnp.transpose(grad, (1, 0, 2)),
        grad_taps,
        grad_weights,
    )


def solution(mesh):
    in_specs = (
        P(None, "phase", "chan"),
        P(),
        P(None, None, None, None, "chan"),
        P(None, "phase", "chan"),
    )
    out_specs = (
        P(None, "phase", "chan"),
        P(None, "phase", "chan"),
        P(),
        P(None, None, None, None, "chan"),
    )
    return jax.shard_map(
        per_device, mesh=mesh, in_specs=in_specs, out_specs=out_specs, check_vma=False
    )
```

time: 651 us -> 260 us (0.40)
  waiting for transfers between devices: 264 us -> 66.4 us
  blocking collectives: 216 us -> 25 us
  starting transfers between devices: 93.6 us -> 138 us
  local copies, waits for them, and re-layouts: 28.6 us -> 8.2 us
  Pallas kernels: 0 us -> 15.3 us
  between operations: 16.5 us -> 1.34 us
  matrix products: 14.9 us -> 0 us
  other arithmetic: 15.3 us -> 2.23 us
    psum x1 -> x0, waiting for transfers between devices: 141 us -> none  [per_device(): grad_kernel = lax.psum(kernel_piece, 'phase').astype(jnp.float32)]
    all_gather x4 -> x0, blocking collectives: 130 us -> none  [per_device(): kernel = lax.all_gather(conv_weights[block_num], 'chan', axis=3, tiled=True)]
    unnamed x3 -> x0, waiting for transfers between devices: 91.4 us -> none
    psum x1 -> x0, blocking collectives: 85.8 us -> none  [per_device(): grad_taps = lax.psum(jnp.stack(tap_grads), ('phase', 'chan'))]
    all_to_all x0 -> x5, starting transfers between devices: none -> 48.3 us  [the longest x2 15.1 us: spread(): return lax.all_to_all(copies, axis, 0, 0, tiled=True)]
    all_to_all x0 -> x1, blocking collectives: none -> 25 us  [per_device(): packed = lax.all_to_all(packed, 'chan', 0, 0, tiled=True)]
    all_to_all x0 -> x5, waiting for transfers between devices: none -> 23.2 us  [the longest x2 22.8 us: spread(): return lax.all_to_all(copies, axis, 0, 0, tiled=True)]
    unnamed x172 -> x48, local copies, waits for them, and re-layouts: 20.6 us -> 3.86 us
  transfers between devices with their start and end apart: 34 -> 37, of which waited for: 15 -> 19; matrix products, arithmetic and copies ran while one was open for 4% -> 1% of each run, Pallas kernels for 0% -> 4%
where the time goes in v1:
time: 260 us; the launch traced here: 256 us
  starting transfers between devices  138 us (53%)
  waiting for transfers between devices  66.4 us (26%)
  blocking collectives  25 us (10%)
  Pallas kernels  15.3 us (6%)
  local copies, waits for them, and re-layouts  8.2 us (3%)
    ppermute x16, starting transfers between devices, beside(): return lax.ppermute(cells, axis, pairs)  45.4 us
    ppermute x16, starting transfers between devices, turned(): lax.ppermute(block, 'phase', [((i - distance) % count, i) for i in range(...  44 us
    ppermute x16, waiting for transfers between devices, beside(): return lax.ppermute(cells, axis, pairs)  32.6 us
    all_to_all x1, blocking collectives, per_device(): packed = lax.all_to_all(packed, 'chan', 0, 0, tiled=True)  25 us
    all_to_all x2, waiting for transfers between devices, spread(): return lax.all_to_all(copies, axis, 0, 0, tiled=True)  22.8 us
    pallas_call x25, Pallas kernels, call(): pl.pallas_call(body, out_shape=out_shape, scratch_shapes=list(scratch), c...  15.3 us
    all_to_all x2, starting transfers between devices, spread(): return lax.all_to_all(copies, axis, 0, 0, tiled=True)  15.1 us
    all_to_all x1, starting transfers between devices, per_device(): early = lax.all_to_all(early, 'phase', 0, 0, tiled=True)  14.2 us
  transfers between devices with their start and end apart: 37, of which 19 were waited for; matrix products, arithmetic and copies ran while one was open for 1% of the time, Pallas kernels for 4%

profile of v1, /device:TPU:7, one launch (start us, length us, event | category | flops | bytes accessed | tf_op | source)
XLA Modules:
  0.0 256.2 jit_solution(10225783887082032649)
XLA Ops:
  2.9 9.3 %all-to-all-start.1 = ((bf16[16,16,1728]{2,1,0:T(8,128)(2,1)}), bf16[16,16,1728]{2,1,0:T(8,128)(2,1)S(1)}, u32[]{:S(2)}, u32[]{:S(2)}) async-start(bf16[16,16,1728]{2,1,0:T(8,128)(2,1)} %broadcast_in_dim.24), calls=%async_computation.1 | async-start | bytes 1835008 | tf_op jit(solution)/shard_map/all_to_all | solution.py:343
  12.4 22.8 %all-to-all-done.1.raw = bf16[16,16,1728]{2,1,0:T(8,128)(2,1)S(1)} async-done(((bf16[16,16,1728]{2,1,0:T(8,128)(2,1)}), bf16[16,16,1728]{2,1,0:T(8,128)(2,1)S(1)}, u32[]{:S(2)}, u32[]{:S(2)}) %all-to-all-start.1) | async-done | bytes 884768 | tf_op jit(solution)/shard_map/all_to_all | solution.py:343
  36.3 5.8 %all-to-all-start = ((bf16[16,16,1728]{2,1,0:T(8,128)(2,1)}), bf16[16,16,1728]{2,1,0:T(8,128)(2,1)S(1)}, u32[]{:S(2)}, u32[]{:S(2)}) async-start(bf16[16,16,1728]{2,1,0:T(8,128)(2,1)} %broadcast_in_dim.21), calls=%async_computation | async-start | bytes 1835008 | tf_op jit(solution)/shard_map/all_to_all | solution.py:343
  48.0 4.0 %collective-permute-start.1 = (bf16[2,64,128]{2,1,0:T(8,128)(2,1)S(1)}, bf16[2,64,128]{2,1,0:T(8,128)(2,1)S(1)}, u32[]{:S(2)}, u32[]{:S(2)}) collective-permute-start(bf16[2,64,128]{2,1,0:T(8,128)(2,1)S(1)} %bitcast.45), channel_id=1, source_target_pairs={{0,1},{1,2},{2,3},{3,4},{4,5},{5,6},{6,7},{7,8},{8,9},{9,10},{10,1... | collective-permute-start | bytes 98312 | tf_op jit(solution)/shard_map/ppermute | solution.py:322
  52.2 6.1 %collective-permute-done = bf16[2,64,128]{2,1,0:T(8,128)(2,1)S(1)} collective-permute-done((bf16[2,64,128]{2,1,0:T(8,128)(2,1)S(1)}, bf16[2,64,128]{2,1,0:T(8,128)(2,1)S(1)}, u32[]{:S(2)}, u32[]{:S(2)}) %collective-permute-start) | collective-permute-done | bytes 32800 | tf_op jit(solution)/shard_map/ppermute | solution.py:322
  58.3 6.7 %collective-permute-done.3 = bf16[2,64,128]{2,1,0:T(8,128)(2,1)S(1)} collective-permute-done((bf16[2,64,128]{2,1,0:T(8,128)(2,1)S(1)}, bf16[2,64,128]{2,1,0:T(8,128)(2,1)S(1)}, u32[]{:S(2)}, u32[]{:S(2)}) %collective-permute-start.3) | collective-permute-done | bytes 32800 | tf_op jit(solution)/shard_map/ppermute | solution.py:322
  66.5 4.0 %collective-permute-start.4 = (bf16[5,2,64,128]{3,2,1,0:T(8,128)(2,1)S(1)}, bf16[5,2,64,128]{3,2,1,0:T(8,128)(2,1)S(1)}, u32[]{:S(2)}, u32[]{:S(2)}) collective-permute-start(bf16[5,2,64,128]{3,2,1,0:T(8,128)(2,1)S(1)} %bitcast_dynamic-update-slice_fusion.1.own), channel_id=1, source_target_pairs={{240,0},{0,16},{16,32},{32,48},{48,64},{64,80},{80,96},{96,112},{1... | collective-permute-start | bytes 491528 | tf_op jit(solution)/shard_map/ppermute | solution.py:331
  70.5 5.1 %collective-permute-start.6 = (bf16[5,1,64,128]{3,2,1,0:T(8,128)(2,1)S(1)}, bf16[5,1,64,128]{3,2,1,0:T(8,128)(2,1)S(1)}, u32[]{:S(2)}, u32[]{:S(2)}) collective-permute-start(bf16[5,1,64,128]{3,2,1,0:T(8,128)(2,1)S(1)} %get-tuple-element.75), channel_id=1, source_target_pairs={{224,0},{240,16},{0,32},{16,48},{32,64},{48,80},{64,96},{80,112},{... | collective-permute-start | bytes 245768 | tf_op jit(solution)/shard_map/ppermute | solution.py:331
  81.4 5.2 %collective-permute-start.8 = (bf16[2,64,128]{2,1,0:T(8,128)(2,1)S(1)}, bf16[2,64,128]{2,1,0:T(8,128)(2,1)S(1)}, u32[]{:S(2)}, u32[]{:S(2)}) collective-permute-start(bf16[2,64,128]{2,1,0:T(8,128)(2,1)S(1)} %get-tuple-element.33.state.rest_1_), channel_id=1, source_target_pairs={{224,0},{240,16},{0,32},{16,48},{32,64},{48,80},{64,96},{80,112},{... | collective-permute-start | bytes 98312 | tf_op jit(solution)/shard_map/ppermute | solution.py:331
  89.2 4.0 %collective-permute-start.10 = (bf16[2,64,128]{2,1,0:T(8,128)(2,1)S(1)}, bf16[2,64,128]{2,1,0:T(8,128)(2,1)S(1)}, u32[]{:S(2)}, u32[]{:S(2)}) collective-permute-start(bf16[2,64,128]{2,1,0:T(8,128)(2,1)S(1)} %shard_map.79.mixed.rest_1_), channel_id=1, source_target_pairs={{0,1},{1,2},{2,3},{3,4},{4,5},{5,6},{6,7},{7,8},{8,9},{9,10},{10,1... | collective-permute-start | bytes 98312 | tf_op jit(solution)/shard_map/ppermute | solution.py:322
  103.6 4.4 %collective-permute-start.14 = (bf16[2,64,128]{2,1,0:T(8,128)(2,1)S(1)}, bf16[2,64,128]{2,1,0:T(8,128)(2,1)S(1)}, u32[]{:S(2)}, u32[]{:S(2)}) collective-permute-start(bf16[2,64,128]{2,1,0:T(8,128)(2,1)S(1)} %shard_map.81.mixed.rest_1_), channel_id=1, source_target_pairs={{0,1},{1,2},{2,3},{3,4},{4,5},{5,6},{6,7},{7,8},{8,9},{9,10},{10,1... | collective-permute-start | bytes 98312 | tf_op jit(solution)/shard_map/ppermute | solution.py:322
  111.5 5.1 %collective-permute-start.16 = (bf16[2,128,128]{2,1,0:T(8,128)(2,1)S(1)}, bf16[2,128,128]{2,1,0:T(8,128)(2,1)S(1)}, u32[]{:S(2)}, u32[]{:S(2)}) collective-permute-start(bf16[2,128,128]{2,1,0:T(8,128)(2,1)S(1)} %get-tuple-element.36.gz), channel_id=1, source_target_pairs={{0,1},{1,2},{2,3},{3,4},{4,5},{5,6},{6,7},{7,8},{8,9},{9,10},{10,1... | collective-permute-start | bytes 196616 | tf_op jit(solution)/shard_map/ppermute | solution.py:322
  118.7 4.2 %collective-permute-start.19 = (bf16[2,64,128]{2,1,0:T(8,128)(2,1)S(1)}, bf16[2,64,128]{2,1,0:T(8,128)(2,1)S(1)}, u32[]{:S(2)}, u32[]{:S(2)}) collective-permute-start(bf16[2,64,128]{2,1,0:T(8,128)(2,1)S(1)} %get-tuple-element.37.low), channel_id=1, source_target_pairs={{64,0},{80,16},{96,32},{112,48},{128,64},{144,80},{160,96},{176,11... | collective-permute-start | bytes 98312 | tf_op jit(solution)/shard_map/ppermute | solution.py:331
  128.6 5.2 %collective-permute-start.20 = (bf16[2,128,128]{2,1,0:T(8,128)(2,1)S(1)}, bf16[2,128,128]{2,1,0:T(8,128)(2,1)S(1)}, u32[]{:S(2)}, u32[]{:S(2)}) collective-permute-start(bf16[2,128,128]{2,1,0:T(8,128)(2,1)S(1)} %get-tuple-element.41.gz), channel_id=1, source_target_pairs={{0,1},{1,2},{2,3},{3,4},{4,5},{5,6},{6,7},{7,8},{8,9},{9,10},{10,1... | collective-permute-start | bytes 196616 | tf_op jit(solution)/shard_map/ppermute | solution.py:322
  137.1 5.4 %collective-permute-start.22 = (bf16[2,64,128]{2,1,0:T(8,128)(2,1)S(1)}, bf16[2,64,128]{2,1,0:T(8,128)(2,1)S(1)}, u32[]{:S(2)}, u32[]{:S(2)}) collective-permute-start(bf16[2,64,128]{2,1,0:T(8,128)(2,1)S(1)} %get-tuple-element.42.low), channel_id=1, source_target_pairs={{224,0},{240,16},{0,32},{16,48},{32,64},{48,80},{64,96},{80,112},{... | collective-permute-start | bytes 98312 | tf_op jit(solution)/shard_map/ppermute | solution.py:331
  146.3 14.2 %all-to-all-start.3 = ((bf16[16,384,128]{2,1,0:T(8,128)(2,1)}), bf16[16,384,128]{2,1,0:T(8,128)(2,1)S(1)}, u32[]{:S(2)}, u32[]{:S(2)}) async-start(bf16[16,384,128]{2,1,0:T(8,128)(2,1)} %pad_maximum_fusion), calls=%async_computation.3 | async-start | bytes 3145728 | tf_op jit(solution)/shard_map/all_to_all | solution.py:433
  161.9 5.0 %collective-permute-start.24 = (bf16[2,128,128]{2,1,0:T(8,128)(2,1)S(1)}, bf16[2,128,128]{2,1,0:T(8,128)(2,1)S(1)}, u32[]{:S(2)}, u32[]{:S(2)}) collective-permute-start(bf16[2,128,128]{2,1,0:T(8,128)(2,1)S(1)} %get-tuple-element.46.gz), channel_id=1, source_target_pairs={{0,1},{1,2},{2,3},{3,4},{4,5},{5,6},{6,7},{7,8},{8,9},{9,10},{10,1... | collective-permute-start | bytes 196616 | tf_op jit(solution)/shard_map/ppermute | solution.py:322
  168.4 13.7 %collective-permute-done.25.right = bf16[2,128,128]{2,1,0:T(8,128)(2,1)S(1)} collective-permute-done((bf16[2,128,128]{2,1,0:T(8,128)(2,1)S(1)}, bf16[2,128,128]{2,1,0:T(8,128)(2,1)S(1)}, u32[]{:S(2)}, u32[]{:S(2)}) %collective-permute-start.25) | collective-permute-done | bytes 65568 | tf_op jit(solution)/shard_map/ppermute | solution.py:322
  184.0 4.4 %collective-permute-start.26 = (bf16[2,64,128]{2,1,0:T(8,128)(2,1)S(1)}, bf16[2,64,128]{2,1,0:T(8,128)(2,1)S(1)}, u32[]{:S(2)}, u32[]{:S(2)}) collective-permute-start(bf16[2,64,128]{2,1,0:T(8,128)(2,1)S(1)} %get-tuple-element.48.low), channel_id=1, source_target_pairs={{240,0},{0,16},{16,32},{32,48},{48,64},{64,80},{80,96},{96,112},{1... | collective-permute-start | bytes 98312 | tf_op jit(solution)/shard_map/ppermute | solution.py:331
  191.5 9.4 %all-to-all-start.2 = ((bf16[16,128,128]{2,1,0:T(8,128)(2,1)}), bf16[16,128,128]{2,1,0:T(8,128)(2,1)S(1)}, u32[]{:S(2)}, u32[]{:S(2)}) async-start(bf16[16,128,128]{2,1,0:T(8,128)(2,1)} %shard_map.93), calls=%async_computation.2 | async-start | bytes 1048576 | tf_op jit(solution)/shard_map/all_to_all | solution.py:435
  202.2 4.0 %collective-permute-start.28 = (bf16[2,128,128]{2,1,0:T(8,128)(2,1)S(1)}, bf16[2,128,128]{2,1,0:T(8,128)(2,1)S(1)}, u32[]{:S(2)}, u32[]{:S(2)}) collective-permute-start(bf16[2,128,128]{2,1,0:T(8,128)(2,1)S(1)} %get-tuple-element.52.gz), channel_id=1, source_target_pairs={{0,1},{1,2},{2,3},{3,4},{4,5},{5,6},{6,7},{7,8},{8,9},{9,10},{10,1... | collective-permute-start | bytes 196616 | tf_op jit(solution)/shard_map/ppermute | solution.py:322
  211.5 25.0 %all_to_all.30.pieces = bf16[16,48,128]{2,1,0:T(8,128)(2,1)S(1)} all-to-all(bf16[16,48,128]{2,1,0:T(8,128)(2,1)S(1)} %shard_map.98), channel_id=1, replica_groups=mesh['phase'=16,'chan'=16] {'chan'}, dimensions={0} | all-to-all | bytes 393216 | tf_op jit(solution)/shard_map/all_to_all | solution.py:459
  237.2 9.6 %all-to-all-start.5 = ((bf16[16,48,128]{2,1,0:T(8,128)(2,1)}), bf16[16,48,128]{2,1,0:T(8,128)(2,1)S(1)}, u32[]{:S(2)}, u32[]{:S(2)}) async-start(bf16[16,48,128]{2,1,0:T(8,128)(2,1)} %shard_map.99), calls=%async_computation.5 | async-start | bytes 393216 | tf_op jit(solution)/shard_map/all_to_all | solution.py:461
  247.2 5.0 %collective-permute-start.30 = (bf16[1,64,128]{2,1,0:T(8,128)(2,1)S(1)}, bf16[1,64,128]{2,1,0:T(8,128)(2,1)S(1)}, u32[]{:S(2)}, u32[]{:S(2)}) collective-permute-start(bf16[1,64,128]{2,1,0:T(8,128)(2,1)S(1)} %get-tuple-element.77), channel_id=1, source_target_pairs={{240,0},{0,16},{16,32},{32,48},{48,64},{64,80},{80,96},{96,112},{1... | collective-permute-start | bytes 49160 | tf_op jit(solution)/shard_map/ppermute | solution.py:331
  (153 shorter events, 67.4 us)
Async XLA Ops:
  2.9 32.3 %all-to-all-start.1 = ((bf16[16,16,1728]{2,1,0:T(8,128)(2,1)}), bf16[16,16,1728]{2,1,0:T(8,128)(2,1)S(1)}, u32[]{:S(2)}, u32[]{:S(2)}) async-start(bf16[16,16,1728]{2,1,0:T(8,128)(2,1)} %broadcast_in_dim.24), calls=%async_computation.1 | async-start | bytes 1835008 | tf_op jit(solution)/shard_map/all_to_all | solution.py:343
  36.3 56.9 %all-to-all-start = ((bf16[16,16,1728]{2,1,0:T(8,128)(2,1)}), bf16[16,16,1728]{2,1,0:T(8,128)(2,1)S(1)}, u32[]{:S(2)}, u32[]{:S(2)}) async-start(bf16[16,16,1728]{2,1,0:T(8,128)(2,1)} %broadcast_in_dim.21), calls=%async_computation | async-start | bytes 1835008 | tf_op jit(solution)/shard_map/all_to_all | solution.py:343
  42.1 16.1 %collective-permute-start = (bf16[2,64,128]{2,1,0:T(8,128)(2,1)S(1)}, bf16[2,64,128]{2,1,0:T(8,128)(2,1)S(1)}, u32[]{:S(2)}, u32[]{:S(2)}) collective-permute-start(bf16[2,64,128]{2,1,0:T(8,128)(2,1)S(1)} %bitcast.42), channel_id=1, source_target_pairs={{0,2},{1,3},{2,4},{3,5},{4,6},{5,7},{6,8},{7,9},{8,10},{9,11},{10,... | collective-permute-start | bytes 98312 | tf_op jit(solution)/shard_map/ppermute | solution.py:322
  45.4 12.9 %collective-permute-start.2 = (bf16[2,64,128]{2,1,0:T(8,128)(2,1)S(1)}, bf16[2,64,128]{2,1,0:T(8,128)(2,1)S(1)}, u32[]{:S(2)}, u32[]{:S(2)}) collective-permute-start(bf16[2,64,128]{2,1,0:T(8,128)(2,1)S(1)} %bitcast.43), channel_id=1, source_target_pairs={{1,0},{2,1},{3,2},{4,3},{5,4},{6,5},{7,6},{8,7},{9,8},{10,9},{11,1... | collective-permute-start | bytes 98312 | tf_op jit(solution)/shard_map/ppermute | solution.py:322
  46.7 18.3 %collective-permute-start.3 = (bf16[2,64,128]{2,1,0:T(8,128)(2,1)S(1)}, bf16[2,64,128]{2,1,0:T(8,128)(2,1)S(1)}, u32[]{:S(2)}, u32[]{:S(2)}) collective-permute-start(bf16[2,64,128]{2,1,0:T(8,128)(2,1)S(1)} %bitcast.44), channel_id=1, source_target_pairs={{2,0},{3,1},{4,2},{5,3},{6,4},{7,5},{8,6},{9,7},{10,8},{11,9},{12,... | collective-permute-start | bytes 98312 | tf_op jit(solution)/shard_map/ppermute | solution.py:322
  48.0 10.2 %collective-permute-start.1 = (bf16[2,64,128]{2,1,0:T(8,128)(2,1)S(1)}, bf16[2,64,128]{2,1,0:T(8,128)(2,1)S(1)}, u32[]{:S(2)}, u32[]{:S(2)}) collective-permute-start(bf16[2,64,128]{2,1,0:T(8,128)(2,1)S(1)} %bitcast.45), channel_id=1, source_target_pairs={{0,1},{1,2},{2,3},{3,4},{4,5},{5,6},{6,7},{7,8},{8,9},{9,10},{10,1... | collective-permute-start | bytes 98312 | tf_op jit(solution)/shard_map/ppermute | solution.py:322
  65.1 12.4 %collective-permute-start.5 = (bf16[5,2,64,128]{3,2,1,0:T(8,128)(2,1)S(1)}, bf16[5,2,64,128]{3,2,1,0:T(8,128)(2,1)S(1)}, u32[]{:S(2)}, u32[]{:S(2)}) collective-permute-start(bf16[5,2,64,128]{3,2,1,0:T(8,128)(2,1)S(1)} %bitcast_dynamic-update-slice_fusion.1.own), channel_id=1, source_target_pairs={{16,0},{32,16},{48,32},{64,48},{80,64},{96,80},{112,96},{128,112},... | collective-permute-start | bytes 491528 | tf_op jit(solution)/shard_map/ppermute | solution.py:331
  66.5 11.0 %collective-permute-start.4 = (bf16[5,2,64,128]{3,2,1,0:T(8,128)(2,1)S(1)}, bf16[5,2,64,128]{3,2,1,0:T(8,128)(2,1)S(1)}, u32[]{:S(2)}, u32[]{:S(2)}) collective-permute-start(bf16[5,2,64,128]{3,2,1,0:T(8,128)(2,1)S(1)} %bitcast_dynamic-update-slice_fusion.1.own), channel_id=1, source_target_pairs={{240,0},{0,16},{16,32},{32,48},{48,64},{64,80},{80,96},{96,112},{1... | collective-permute-start | bytes 491528 | tf_op jit(solution)/shard_map/ppermute | solution.py:331
  70.4 7.0 %collective-permute-start.7 = (bf16[5,1,64,128]{3,2,1,0:T(8,128)(2,1)S(1)}, bf16[5,1,64,128]{3,2,1,0:T(8,128)(2,1)S(1)}, u32[]{:S(2)}, u32[]{:S(2)}) collective-permute-start(bf16[5,1,64,128]{3,2,1,0:T(8,128)(2,1)S(1)} %get-tuple-element.74), channel_id=1, source_target_pairs={{32,0},{48,16},{64,32},{80,48},{96,64},{112,80},{128,96},{144,112}... | collective-permute-start | bytes 245768 | tf_op jit(solution)/shard_map/ppermute | solution.py:331
  70.5 6.9 %collective-permute-start.6 = (bf16[5,1,64,128]{3,2,1,0:T(8,128)(2,1)S(1)}, bf16[5,1,64,128]{3,2,1,0:T(8,128)(2,1)S(1)}, u32[]{:S(2)}, u32[]{:S(2)}) collective-permute-start(bf16[5,1,64,128]{3,2,1,0:T(8,128)(2,1)S(1)} %get-tuple-element.75), channel_id=1, source_target_pairs={{224,0},{240,16},{0,32},{16,48},{32,64},{48,80},{64,96},{80,112},{... | collective-permute-start | bytes 245768 | tf_op jit(solution)/shard_map/ppermute | solution.py:331
  94.6 6.8 %collective-permute-start.13 = (bf16[2,64,128]{2,1,0:T(8,128)(2,1)S(1)}, bf16[2,64,128]{2,1,0:T(8,128)(2,1)S(1)}, u32[]{:S(2)}, u32[]{:S(2)}) collective-permute-start(bf16[2,64,128]{2,1,0:T(8,128)(2,1)S(1)} %get-tuple-element.34.state.rest_1_), channel_id=1, source_target_pairs={{64,0},{80,16},{96,32},{112,48},{128,64},{144,80},{160,96},{176,11... | collective-permute-start | bytes 98312 | tf_op jit(solution)/shard_map/ppermute | solution.py:331
  110.2 7.7 %collective-permute-start.17 = (bf16[2,128,128]{2,1,0:T(8,128)(2,1)S(1)}, bf16[2,128,128]{2,1,0:T(8,128)(2,1)S(1)}, u32[]{:S(2)}, u32[]{:S(2)}) collective-permute-start(bf16[2,128,128]{2,1,0:T(8,128)(2,1)S(1)} %get-tuple-element.36.gz), channel_id=1, source_target_pairs={{1,0},{2,1},{3,2},{4,3},{5,4},{6,5},{7,6},{8,7},{9,8},{10,9},{11,1... | collective-permute-start | bytes 196616 | tf_op jit(solution)/shard_map/ppermute | solution.py:322
  118.7 6.8 %collective-permute-start.19 = (bf16[2,64,128]{2,1,0:T(8,128)(2,1)S(1)}, bf16[2,64,128]{2,1,0:T(8,128)(2,1)S(1)}, u32[]{:S(2)}, u32[]{:S(2)}) collective-permute-start(bf16[2,64,128]{2,1,0:T(8,128)(2,1)S(1)} %get-tuple-element.37.low), channel_id=1, source_target_pairs={{64,0},{80,16},{96,32},{112,48},{128,64},{144,80},{160,96},{176,11... | collective-permute-start | bytes 98312 | tf_op jit(solution)/shard_map/ppermute | solution.py:331
  135.9 7.8 %collective-permute-start.23 = (bf16[2,64,128]{2,1,0:T(8,128)(2,1)S(1)}, bf16[2,64,128]{2,1,0:T(8,128)(2,1)S(1)}, u32[]{:S(2)}, u32[]{:S(2)}) collective-permute-start(bf16[2,64,128]{2,1,0:T(8,128)(2,1)S(1)} %get-tuple-element.42.low), channel_id=1, source_target_pairs={{32,0},{48,16},{64,32},{80,48},{96,64},{112,80},{128,96},{144,112}... | collective-permute-start | bytes 98312 | tf_op jit(solution)/shard_map/ppermute | solution.py:331
  137.1 6.6 %collective-permute-start.22 = (bf16[2,64,128]{2,1,0:T(8,128)(2,1)S(1)}, bf16[2,64,128]{2,1,0:T(8,128)(2,1)S(1)}, u32[]{:S(2)}, u32[]{:S(2)}) collective-permute-start(bf16[2,64,128]{2,1,0:T(8,128)(2,1)S(1)} %get-tuple-element.42.low), channel_id=1, source_target_pairs={{224,0},{240,16},{0,32},{16,48},{32,64},{48,80},{64,96},{80,112},{... | collective-permute-start | bytes 98312 | tf_op jit(solution)/shard_map/ppermute | solution.py:331
  146.3 45.2 %all-to-all-start.3 = ((bf16[16,384,128]{2,1,0:T(8,128)(2,1)}), bf16[16,384,128]{2,1,0:T(8,128)(2,1)S(1)}, u32[]{:S(2)}, u32[]{:S(2)}) async-start(bf16[16,384,128]{2,1,0:T(8,128)(2,1)} %pad_maximum_fusion), calls=%async_computation.3 | async-start | bytes 3145728 | tf_op jit(solution)/shard_map/all_to_all | solution.py:433
  160.5 21.6 %collective-permute-start.25 = (bf16[2,128,128]{2,1,0:T(8,128)(2,1)S(1)}, bf16[2,128,128]{2,1,0:T(8,128)(2,1)S(1)}, u32[]{:S(2)}, u32[]{:S(2)}) collective-permute-start(bf16[2,128,128]{2,1,0:T(8,128)(2,1)S(1)} %get-tuple-element.46.gz), channel_id=1, source_target_pairs={{1,0},{2,1},{3,2},{4,3},{5,4},{6,5},{7,6},{8,7},{9,8},{10,9},{11,1... | collective-permute-start | bytes 196616 | tf_op jit(solution)/shard_map/ppermute | solution.py:322
  161.9 20.2 %collective-permute-start.24 = (bf16[2,128,128]{2,1,0:T(8,128)(2,1)S(1)}, bf16[2,128,128]{2,1,0:T(8,128)(2,1)S(1)}, u32[]{:S(2)}, u32[]{:S(2)}) collective-permute-start(bf16[2,128,128]{2,1,0:T(8,128)(2,1)S(1)} %get-tuple-element.46.gz), channel_id=1, source_target_pairs={{0,1},{1,2},{2,3},{3,4},{4,5},{5,6},{6,7},{7,8},{8,9},{9,10},{10,1... | collective-permute-start | bytes 196616 | tf_op jit(solution)/shard_map/ppermute | solution.py:322
  182.9 7.0 %collective-permute-start.27 = (bf16[2,64,128]{2,1,0:T(8,128)(2,1)S(1)}, bf16[2,64,128]{2,1,0:T(8,128)(2,1)S(1)}, u32[]{:S(2)}, u32[]{:S(2)}) collective-permute-start(bf16[2,64,128]{2,1,0:T(8,128)(2,1)S(1)} %get-tuple-element.48.low), channel_id=1, source_target_pairs={{16,0},{32,16},{48,32},{64,48},{80,64},{96,80},{112,96},{128,112},... | collective-permute-start | bytes 98312 | tf_op jit(solution)/shard_map/ppermute | solution.py:331
  191.5 19.8 %all-to-all-start.2 = ((bf16[16,128,128]{2,1,0:T(8,128)(2,1)}), bf16[16,128,128]{2,1,0:T(8,128)(2,1)S(1)}, u32[]{:S(2)}, u32[]{:S(2)}) async-start(bf16[16,128,128]{2,1,0:T(8,128)(2,1)} %shard_map.93), calls=%async_computation.2 | async-start | bytes 1048576 | tf_op jit(solution)/shard_map/all_to_all | solution.py:435
  200.9 7.3 %collective-permute-start.29 = (bf16[2,128,128]{2,1,0:T(8,128)(2,1)S(1)}, bf16[2,128,128]{2,1,0:T(8,128)(2,1)S(1)}, u32[]{:S(2)}, u32[]{:S(2)}) collective-permute-start(bf16[2,128,128]{2,1,0:T(8,128)(2,1)S(1)} %get-tuple-element.52.gz), channel_id=1, source_target_pairs={{1,0},{2,1},{3,2},{4,3},{5,4},{6,5},{7,6},{8,7},{9,8},{10,9},{11,1... | collective-permute-start | bytes 196616 | tf_op jit(solution)/shard_map/ppermute | solution.py:322
  202.2 7.4 %collective-permute-start.28 = (bf16[2,128,128]{2,1,0:T(8,128)(2,1)S(1)}, bf16[2,128,128]{2,1,0:T(8,128)(2,1)S(1)}, u32[]{:S(2)}, u32[]{:S(2)}) collective-permute-start(bf16[2,128,128]{2,1,0:T(8,128)(2,1)S(1)} %get-tuple-element.52.gz), channel_id=1, source_target_pairs={{0,1},{1,2},{2,3},{3,4},{4,5},{5,6},{6,7},{7,8},{8,9},{9,10},{10,1... | collective-permute-start | bytes 196616 | tf_op jit(solution)/shard_map/ppermute | solution.py:322
  237.2 17.3 %all-to-all-start.5 = ((bf16[16,48,128]{2,1,0:T(8,128)(2,1)}), bf16[16,48,128]{2,1,0:T(8,128)(2,1)S(1)}, u32[]{:S(2)}, u32[]{:S(2)}) async-start(bf16[16,48,128]{2,1,0:T(8,128)(2,1)} %shard_map.99), calls=%async_computation.5 | async-start | bytes 393216 | tf_op jit(solution)/shard_map/all_to_all | solution.py:461
  246.8 6.9 %collective-permute-start.31 = (bf16[1,64,128]{2,1,0:T(8,128)(2,1)S(1)}, bf16[1,64,128]{2,1,0:T(8,128)(2,1)S(1)}, u32[]{:S(2)}, u32[]{:S(2)}) collective-permute-start(bf16[1,64,128]{2,1,0:T(8,128)(2,1)S(1)} %get-tuple-element.76), channel_id=1, source_target_pairs={{16,0},{32,16},{48,32},{64,48},{80,64},{96,80},{112,96},{128,112},... | collective-permute-start | bytes 49160 | tf_op jit(solution)/shard_map/ppermute | solution.py:331
  (32 other events, 445.7 us)

commit v2 on v1

--- a/solution.py
+++ b/solution.py
@@ -68,19 +68,19 @@
                 columns[start : start + rows, t * CELLS : (t + 1) * CELLS] = piece
 
 
-def sort_matrix(transposed):
+def permutation(wanted):
     r = lax.broadcasted_iota(jnp.int32, (128, 128), 0)
     c = lax.broadcasted_iota(jnp.int32, (128, 128), 1)
-    if transposed:
-        r, c = c, r
-    wanted = (r % 64) // 4 * 8 + r // 64 * 4 + r % 4
-    return jnp.where(c == wanted, 1.0, 0.0).astype(bf16)
-
-
-def sort_kernel(raw, out):
-    order = sort_matrix(False)
-    for n in range(2):
-        rows = raw[:, 8 * n : 8 * n + 8, :].reshape(128, DEPTH)
+    return jnp.where(wanted(r) == c, 1.0, 0.0).astype(bf16)
+
+
+def sort_kernel(half, odd, mine, other, out):
+    order = permutation(lambda r: r % 64 // 4 * 8 + r // 64 * 4 + r % 4)
+    keep = (odd[:1, :1] > 0.5) if half else (odd[:1, :1] < 0.5)
+    for n in range(2):
+        here = mine[:, 8 * n : 8 * n + 8, :].reshape(128, DEPTH)
+        there = other[:, 8 * n : 8 * n + 8, :].reshape(128, DEPTH)
+        rows = jnp.where(keep, here.astype(f32), there.astype(f32)).astype(bf16)
         out[n] = jnp.dot(order, rows, preferred_element_type=f32).astype(bf16)
 
 
@@ -112,16 +112,33 @@
         out[n] = mix(t, behind[n], state[n], ahead[n])
 
 
-def front_mix_kernel(taps, own, back1, next1, back2, next2, mixed, line):
+def wide_columns(columns, planes):
+    masks = inside_masks(1)
+    for x, units in enumerate(planes):
+        for q, unit in enumerate(units):
+            for kk, piece in enumerate(spread_unit(unit, masks, 1)):
+                columns[x, kk * CHANS : (kk + 1) * CHANS, q * CELLS : (q + 1) * CELLS] = piece
+
+
+def wide_conv(weight, columns, x):
+    third = 9 * CHANS
+    total = None
+    for dx in range(3):
+        part = jnp.dot(
+            weight[:, dx * third : (dx + 1) * third], columns[x + dx], preferred_element_type=f32
+        )
+        total = part if dx == 0 else total + part
+    return total
+
+
+def front_mix_kernel(taps, *refs):
+    planes, (mixed, line) = refs[:5], refs[5:]
     t = tap_columns(taps, 0)
     for x in range(5):
-        f = [back2[x, 0], back1[x, 0], back1[x, 1], own[x, 0], own[x, 1]]
-        f += [next1[x, 0], next1[x, 1], next2[x, 0]]
         for q in range(6):
-            mixed[x, q] = mix(t, f[q], f[q + 1], f[q + 2])
-        if x == 2:
-            for q in range(4):
-                line[q] = f[q + 2]
+            mixed[x, q] = mix(t, planes[x][q], planes[x][q + 1], planes[x][q + 2])
+    for q in range(4):
+        line[q] = planes[2][q + 2]
 
 
 def gated_sum(conv, n):
@@ -131,31 +148,19 @@
 
 
 def front_kernel(
-    edge, taps, weights, mixed, own, back1, next1,
+    edge, taps, weights, mixed, before, own, after_own,
     value0, gate0, line1, mixed1, value1, gate1, after, columns, narrow,
 ):
-    masks = inside_masks(1)
-    for x in range(5):
-        for q in range(6):
-            for kk, piece in enumerate(spread_unit(mixed[x, q], masks, 1)):
-                columns[x, kk * CHANS : (kk + 1) * CHANS, q * CELLS : (q + 1) * CELLS] = piece
+    wide_columns(columns, [[mixed[x, q] for q in range(6)] for x in range(5)])
     t = tap_columns(taps, 1)
-    third = 9 * CHANS
     planes = []
     for x in range(3):
-        conv = jnp.zeros((2 * CHANS, 6 * CELLS), f32)
-        for dx in range(3):
-            conv = conv + jnp.dot(
-                weights[0, :, dx * third : (dx + 1) * third],
-                columns[x + dx],
-                preferred_element_type=f32,
-            )
-        f = [back1[x + 1, 0], back1[x + 1, 1], own[x + 1, 0], own[x + 1, 1]]
-        f += [next1[x + 1, 0], next1[x + 1, 1]]
+        conv = wide_conv(weights[0], columns, x)
+        f = (before, own, after_own)[x]
         states = []
         for q in range(6):
             v, s = gated_sum(conv, q)
-            state = f[q].astype(f32) + v * s
+            state = f[q + 1].astype(f32) + v * s
             if x == 1:
                 state = state.astype(bf16)
                 line1[q] = state
@@ -179,19 +184,23 @@
         after[n] = (line1[n + 2].astype(f32) + v * s).astype(bf16)
 
 
-def conv_kernel(which, weights, mixed, left, right, state, *rest):
-    fill_columns(rest[-1], [[a[0], a[1]] for a in (left, mixed, right)], 1)
-    conv = jnp.dot(weights[which], rest[-1][...], preferred_element_type=f32)
+def conv_kernel(weights, mixed, left, right, state, value, gate, after, columns):
+    fill_columns(columns, [[a[0], a[1]] for a in (left, mixed, right)], 1)
+    conv = jnp.dot(weights[0], columns[...], preferred_element_type=f32)
     for n in range(2):
         v, s = gated_sum(conv, n)
-        after = (state[n].astype(f32) + v * s).astype(bf16)
-        if which == 0:
-            rest[0][n] = v
-            rest[1][n] = s
-            rest[2][n] = after
-        else:
-            rest[1][n, :CHANS], rest[1][n, CHANS:] = gated(rest[0][n].astype(f32), v, s)
-            rest[2][n] = after
+        value[n] = v
+        gate[n] = s
+        after[n] = (state[n].astype(f32) + v * s).astype(bf16)
+
+
+def turn_kernel(weights, mixed, left, right, state, grad, gz, after, columns):
+    fill_columns(columns, [[a[0], a[1]] for a in (left, mixed, right)], 1)
+    conv = jnp.dot(weights[1], columns[...], preferred_element_type=f32)
+    for n in range(2):
+        v, s = gated_sum(conv, n)
+        gz[n, :CHANS], gz[n, CHANS:] = gated(grad[n].astype(f32), v, s)
+        after[n] = (state[n].astype(f32) + v * s).astype(bf16)
 
 
 def gated(y, v, s):
@@ -224,6 +233,9 @@
 
 def weight_kernel(offsets, gz, *rest):
     sources, (out, columns) = rest[:-2], rest[-2:]
+    if len(sources) == 2:
+        sources, held = sources[:1], sources[1]
+        out[:, 128:] = held[...]
     if len(sources) == 1:
         x, t = offsets
         planes = [[sources[0][x + n, t], sources[0][x + n, t + 1]] for n in range(3)]
@@ -231,14 +243,15 @@
         planes = [[a[0], a[1]] for a in sources]
     fill_columns(columns, planes, 1)
     both = jnp.concatenate([gz[0], gz[1]], axis=1)
-    both = jnp.dot(sort_matrix(True), both, preferred_element_type=f32).astype(bf16)
+    order = permutation(lambda r: r % 8 // 4 * 64 + r // 8 * 4 + r % 4)
+    both = jnp.dot(order, both, preferred_element_type=f32).astype(bf16)
     grad = lax.dot_general(
         columns[...], both, (((1,), (1,)), ((), ())), preferred_element_type=f32
     )
-    out[:13] = grad[: 13 * 128].astype(bf16).reshape(13, 128, 128)
+    out[:13, :128] = grad[: 13 * 128].astype(bf16).reshape(13, 128, 128)
     out[13, :CHANS] = grad[13 * 128 :].astype(bf16)
-    out[13, CHANS:] = jnp.zeros((CHANS, 128), bf16)
-    out[14:] = jnp.zeros((2, 128, 128), bf16)
+    out[13, CHANS:128] = jnp.zeros((CHANS, 128), bf16)
+    out[14:, :128] = jnp.zeros((2, 128, 128), bf16)
 
 
 def turned_sum(pieces, start):
@@ -254,19 +267,14 @@
     return swapped.astype(bf16)
 
 
-def part_kernel(pieces, out):
-    for n in range(3):
-        out[2 - n] = turned_sum(pieces, 128 * n)
-
-
 def halves(value):
     high = value.astype(bf16)
     low = (value - high.astype(f32)).astype(bf16)
     return high, low
 
 
-def pack_kernel(pieces, later, taps, out):
-    parts = [turned_sum(pieces, 0), later[0], later[1], later[2]]
+def pack_kernel(pieces, taps, out):
+    parts = [turned_sum(pieces, start) for start in (0, 384, 256, 128)]
     high, low = halves(taps[...])
     for j in range(16):
         for b in range(BLOCKS):
@@ -358,19 +366,26 @@
     edge = jnp.stack([place > 0, place < groups - 1]).astype(f32)
     edge = jnp.broadcast_to(edge[:, None], (2, CELLS))
 
-    raw = []
-    for n in range(2):
-        raw.append(spread(rows[2 * n : 2 * n + 2].reshape(4 * own, DEPTH), "chan"))
-    weights = [call(sort_kernel, shaped((2, 128, DEPTH), bf16), r) for r in raw]
-
-    cells = [beside(state, "chan", d) for d in (2, 1, -1, -2)]
-    here = jnp.stack([cells[0], cells[1], state, cells[2], cells[3]])
-    back1, next1 = turned(here, 1), turned(here, -1)
-    back2, next2 = turned(here[:, 1:], 2), turned(here[:, :1], -2)
+    odd = lax.axis_index("phase") % 2
+    rows = lax.dynamic_slice_in_dim(rows.reshape(2, 4 * own, DEPTH), odd, 1, axis=0)[0]
+    mine = spread(rows, "chan")
+    count = lax.axis_size("phase")
+    other = lax.ppermute(mine, "phase", [(i, i ^ 1) for i in range(count)])
+    odd = jnp.broadcast_to(odd.astype(f32), (8, 128))
+    weights = [
+        call(functools.partial(sort_kernel, n), shaped((2, 128, DEPTH), bf16), odd, mine, other)
+        for n in range(2)
+    ]
+
+    around = [turned(state[1:], 2), turned(state, 1), state, turned(state, -1)]
+    around.append(turned(state[:1], -2))
+    line = jnp.concatenate(around)
+    cells = [beside(line, "chan", d) for d in (2, 1, -1, -2)]
+    cells.insert(2, line)
     mixed0, line0 = call(
-      front_mix_kernel,
-      [shaped((5, 6, CHANS, CELLS), bf16), shaped((4, CHANS, CELLS), bf16)],
-      taps, here, back1, next1, back2, next2,
+        front_mix_kernel,
+        [shaped((5, 6, CHANS, CELLS), bf16), shaped((4, CHANS, CELLS), bf16)],
+        taps, *cells,
     )
     value0, gate0, line1, mixed1, value1, gate1, state = call(
         front_kernel,
@@ -383,7 +398,7 @@
             shaped(unit, f32),
             shaped(unit, bf16),
         ],
-        edge, taps, weights[0], mixed0, here, back1, next1,
+        edge, taps, weights[0], mixed0, *cells[1:4],
         scratch=[pltpu.VMEM((5, 9 * CHANS, 6 * CELLS), bf16), columns],
     )
     saved = [
@@ -399,20 +414,20 @@
         left, right = sides(mixed, "chan")
         if b < BLOCKS - 1:
             value, gate, state = call(
-                functools.partial(conv_kernel, 0),
+                conv_kernel,
                 [shaped(unit, f32), shaped(unit, f32), shaped(unit, bf16)],
                 weights[1], mixed, left, right, state,
                 scratch=[columns],
             )
-            saved.append(((behind, prior, ahead), (left, mixed, right), None, value, gate))
         else:
             gz, state = call(
-                functools.partial(conv_kernel, 1),
+                turn_kernel,
                 [shaped(gunit, bf16), shaped(unit, bf16)],
                 weights[1], mixed, left, right, state, grad,
                 scratch=[columns],
             )
-            saved.append(((behind, prior, ahead), (left, mixed, right), None, None, None))
+            value = gate = None
+        saved.append(((behind, prior, ahead), (left, mixed, right), None, value, gate))
     final = state
     backs = [call(flip_kernel, shaped((2, CHANS, 2 * DEPTH), bf16), w) for w in weights]
 
@@ -421,16 +436,14 @@
     for b in reversed(range(BLOCKS)):
         line, mixed, offsets, _, _ = saved[b]
         gleft, gright = sides(gz, "chan")
+        extra = [jnp.concatenate(held, axis=1)] if b == 0 else []
         pieces = call(
             functools.partial(weight_kernel, offsets),
-            shaped((16, 128, 128), bf16),
-            gz, *mixed,
+            shaped((16, 128 + 384 * len(extra), 128), bf16),
+            gz, *mixed, *extra,
             scratch=[columns],
         )
         held.append(pieces)
-        if b == 1:
-            early = jnp.concatenate(held, axis=1)
-            early = lax.all_to_all(early, "phase", 0, 0, tiled=True)
         if b == 0:
             late = lax.all_to_all(pieces, "phase", 0, 0, tiled=True)
         low, tap_grads[b] = call(
@@ -452,10 +465,9 @@
                 [shaped(unit, bf16), shaped(gunit, bf16)],
                 taps, grad, low, behind, ahead, saved[b - 1][3], saved[b - 1][4],
             )
-    parts = call(part_kernel, shaped((3, 128, 128), bf16), early)
     tap_rows = jnp.concatenate(tap_grads, axis=1).T.reshape(6, 2 * CHANS)
     tap_rows = jnp.pad(tap_rows, [(0, 2), (0, 0)])
-    packed = call(pack_kernel, shaped((16, 48, 128), bf16), late, parts, tap_rows)
+    packed = call(pack_kernel, shaped((16, 48, 128), bf16), late, tap_rows)
     packed = lax.all_to_all(packed, "chan", 0, 0, tiled=True)
     packed = call(repack_kernel, shaped((16, 48, 128), bf16), packed)
     packed = lax.all_to_all(packed, "phase", 0, 0, tiled=True)

time: 260 us -> 240 us (0.923); the launches traced: 256 us -> 239 us
  starting transfers between devices: 138 us -> 93.9 us
  waiting for transfers between devices: 66.4 us -> 106 us
  blocking collectives: 25 us -> 16 us
    ppermute x16, waiting for transfers between devices: 10.6 us -> 38.3 us  [turned(): lax.ppermute(block, 'phase', [((i - distance) % count, i) for i in range(...]
    all_to_all x1 -> x0, starting transfers between devices: 14.2 us -> none  [per_device(): early = lax.all_to_all(early, 'phase', 0, 0, tiled=True)]
    ppermute x16, starting transfers between devices: 45.4 us -> 32.2 us  [beside(): return lax.ppermute(cells, axis, pairs)]
    ppermute x16, waiting for transfers between devices: 32.6 us -> 44.6 us  [beside(): return lax.ppermute(cells, axis, pairs)]
    ppermute x16, starting transfers between devices: 44 us -> 33.5 us  [turned(): lax.ppermute(block, 'phase', [((i - distance) % count, i) for i in range(...]
    all_to_all x1, blocking collectives: 25 us -> 16 us  [per_device(): packed = lax.all_to_all(packed, 'chan', 0, 0, tiled=True)]
    all_to_all x2 -> x1, starting transfers between devices: 15.1 us -> 9.3 us  [spread(): return lax.all_to_all(copies, axis, 0, 0, tiled=True)]
    ppermute x0 -> x1, starting transfers between devices: none -> 3.76 us  [per_device(): other = lax.ppermute(mine, 'phase', [(i, i ^ 1) for i in range(count)])]
  transfers between devices with their start and end apart: 37 -> 36, of which waited for: 19 -> 24; matrix products, arithmetic and copies ran while one was open for 1% -> 1% of each run, Pallas kernels for 4% -> 3%
where the time goes in v2:
time: 240 us; the launch traced here: 239 us
  waiting for transfers between devices  106 us (44%)
  starting transfers between devices  93.9 us (39%)
  blocking collectives  16 us (7%)
  Pallas kernels  14.9 us (6%)
  local copies, waits for them, and re-layouts  6.38 us (3%)
    ppermute x16, waiting for transfers between devices, beside(): return lax.ppermute(cells, axis, pairs)  44.6 us
    ppermute x16, waiting for transfers between devices, turned(): lax.ppermute(block, 'phase', [((i - distance) % count, i) for i in range(...  38.3 us
    ppermute x16, starting transfers between devices, turned(): lax.ppermute(block, 'phase', [((i - distance) % count, i) for i in range(...  33.5 us
    ppermute x16, starting transfers between devices, beside(): return lax.ppermute(cells, axis, pairs)  32.2 us
    all_to_all x1, waiting for transfers between devices, spread(): return lax.all_to_all(copies, axis, 0, 0, tiled=True)  23 us
    all_to_all x1, blocking collectives, per_device(): packed = lax.all_to_all(packed, 'chan', 0, 0, tiled=True)  16 us
    pallas_call x24, Pallas kernels, call(): pl.pallas_call(body, out_shape=out_shape, scratch_shapes=list(scratch), c...  14.9 us
    all_to_all x1, starting transfers between devices, spread(): return lax.all_to_all(copies, axis, 0, 0, tiled=True)  9.3 us
  transfers between devices with their start and end apart: 36, of which 24 were waited for; matrix products, arithmetic and copies ran while one was open for 1% of the time, Pallas kernels for 3%

profile of v2, /device:TPU:7, one launch (start us, length us, event | category | flops | bytes accessed | tf_op | source)
XLA Modules:
  0.0 239.3 jit_solution(8102738953825644082)
XLA Ops:
  3.0 9.3 %all-to-all-start = ((bf16[16,16,1728]{2,1,0:T(8,128)(2,1)}), bf16[16,16,1728]{2,1,0:T(8,128)(2,1)S(1)}, u32[]{:S(2)}, u32[]{:S(2)}) async-start(bf16[16,16,1728]{2,1,0:T(8,128)(2,1)} %broadcast_in_dim.18), calls=%async_computation | async-start | bytes 1835008 | tf_op jit(solution)/shard_map/all_to_all | solution.py:351
  12.3 23.0 %all-to-all-done.mine = bf16[16,16,1728]{2,1,0:T(8,128)(2,1)S(1)} async-done(((bf16[16,16,1728]{2,1,0:T(8,128)(2,1)}), bf16[16,16,1728]{2,1,0:T(8,128)(2,1)S(1)}, u32[]{:S(2)}, u32[]{:S(2)}) %all-to-all-start) | async-done | bytes 884768 | tf_op jit(solution)/shard_map/all_to_all | solution.py:351
  35.3 3.8 %collective-permute-start = (bf16[16,16,1728]{2,1,0:T(8,128)(2,1)S(1)}, bf16[16,16,1728]{2,1,0:T(8,128)(2,1)S(1)}, u32[]{:S(2)}, u32[]{:S(2)}) collective-permute-start(bf16[16,16,1728]{2,1,0:T(8,128)(2,1)S(1)} %all-to-all-done.mine), channel_id=1, source_target_pairs={{0,16},{16,0},{32,48},{48,32},{64,80},{80,64},{96,112},{112,96},{1... | collective-permute-start | bytes 2654216 | tf_op jit(solution)/shard_map/ppermute | solution.py:373
  44.0 5.9 %collective-permute-done.3 = bf16[2,64,128]{2,1,0:T(8,128)(2,1)S(1)} collective-permute-done((bf16[2,64,128]{2,1,0:T(8,128)(2,1)S(1)}, bf16[2,64,128]{2,1,0:T(8,128)(2,1)S(1)}, u32[]{:S(2)}, u32[]{:S(2)}) %collective-permute-start.3) | collective-permute-done | bytes 32800 | tf_op jit(solution)/shard_map/ppermute | solution.py:339
  55.8 4.1 %collective-permute-done.7.refs_3_.after_own = bf16[8,64,128]{2,1,0:T(8,128)(2,1)S(1)} collective-permute-done((bf16[8,64,128]{2,1,0:T(8,128)(2,1)S(1)}, bf16[8,64,128]{2,1,0:T(8,128)(2,1)S(1)}, u32[]{:S(2)}, u32[]{:S(2)}) %collective-permute-start.7) | collective-permute-done | bytes 131104 | tf_op jit(solution)/shard_map/ppermute | solution.py:330
  59.9 4.4 %collective-permute-done.8.refs_4_ = bf16[8,64,128]{2,1,0:T(8,128)(2,1)S(1)} collective-permute-done((bf16[8,64,128]{2,1,0:T(8,128)(2,1)S(1)}, bf16[8,64,128]{2,1,0:T(8,128)(2,1)S(1)}, u32[]{:S(2)}, u32[]{:S(2)}) %collective-permute-start.8) | collective-permute-done | bytes 131104 | tf_op jit(solution)/shard_map/ppermute | solution.py:330
  70.6 3.7 %collective-permute-done.10.ahead.rest_2_ = bf16[2,64,128]{2,1,0:T(8,128)(2,1)S(1)} collective-permute-done((bf16[2,64,128]{2,1,0:T(8,128)(2,1)S(1)}, bf16[2,64,128]{2,1,0:T(8,128)(2,1)S(1)}, u32[]{:S(2)}, u32[]{:S(2)}) %collective-permute-start.10) | collective-permute-done | bytes 32800 | tf_op jit(solution)/shard_map/ppermute | solution.py:339
  77.6 5.0 %collective-permute-done.12.right.rest_2_ = bf16[2,64,128]{2,1,0:T(8,128)(2,1)S(1)} collective-permute-done((bf16[2,64,128]{2,1,0:T(8,128)(2,1)S(1)}, bf16[2,64,128]{2,1,0:T(8,128)(2,1)S(1)}, u32[]{:S(2)}, u32[]{:S(2)}) %collective-permute-start.12) | collective-permute-done | bytes 32800 | tf_op jit(solution)/shard_map/ppermute | solution.py:330
  83.2 3.0 %collective-permute-start.14 = (bf16[2,64,128]{2,1,0:T(8,128)(2,1)S(1)}, bf16[2,64,128]{2,1,0:T(8,128)(2,1)S(1)}, u32[]{:S(2)}, u32[]{:S(2)}) collective-permute-start(bf16[2,64,128]{2,1,0:T(8,128)(2,1)S(1)} %get-tuple-element.34.state.rest_1_), channel_id=1, source_target_pairs={{64,0},{80,16},{96,32},{112,48},{128,64},{144,80},{160,96},{176,11... | collective-permute-start | bytes 98312 | tf_op jit(solution)/shard_map/ppermute | solution.py:339
  90.0 4.3 %collective-permute-start.15 = (bf16[2,64,128]{2,1,0:T(8,128)(2,1)S(1)}, bf16[2,64,128]{2,1,0:T(8,128)(2,1)S(1)}, u32[]{:S(2)}, u32[]{:S(2)}) collective-permute-start(bf16[2,64,128]{2,1,0:T(8,128)(2,1)S(1)} %shard_map.81.mixed.rest_1_), channel_id=1, source_target_pairs={{0,1},{1,2},{2,3},{3,4},{4,5},{5,6},{6,7},{7,8},{8,9},{9,10},{10,1... | collective-permute-start | bytes 98312 | tf_op jit(solution)/shard_map/ppermute | solution.py:330
  95.8 3.1 %collective-permute-done.16.right.rest_2_ = bf16[2,64,128]{2,1,0:T(8,128)(2,1)S(1)} collective-permute-done((bf16[2,64,128]{2,1,0:T(8,128)(2,1)S(1)}, bf16[2,64,128]{2,1,0:T(8,128)(2,1)S(1)}, u32[]{:S(2)}, u32[]{:S(2)}) %collective-permute-start.16) | collective-permute-done | bytes 32800 | tf_op jit(solution)/shard_map/ppermute | solution.py:330
  112.5 2.9 %collective-permute-done.20.ahead = bf16[2,64,128]{2,1,0:T(8,128)(2,1)S(1)} collective-permute-done((bf16[2,64,128]{2,1,0:T(8,128)(2,1)S(1)}, bf16[2,64,128]{2,1,0:T(8,128)(2,1)S(1)}, u32[]{:S(2)}, u32[]{:S(2)}) %collective-permute-start.20) | collective-permute-done | bytes 32800 | tf_op jit(solution)/shard_map/ppermute | solution.py:339
  119.2 3.8 %collective-permute-done.22.right = bf16[2,128,128]{2,1,0:T(8,128)(2,1)S(1)} collective-permute-done((bf16[2,128,128]{2,1,0:T(8,128)(2,1)S(1)}, bf16[2,128,128]{2,1,0:T(8,128)(2,1)S(1)}, u32[]{:S(2)}, u32[]{:S(2)}) %collective-permute-start.22) | collective-permute-done | bytes 65568 | tf_op jit(solution)/shard_map/ppermute | solution.py:330
  126.6 4.8 %collective-permute-done.24.ahead = bf16[2,64,128]{2,1,0:T(8,128)(2,1)S(1)} collective-permute-done((bf16[2,64,128]{2,1,0:T(8,128)(2,1)S(1)}, bf16[2,64,128]{2,1,0:T(8,128)(2,1)S(1)}, u32[]{:S(2)}, u32[]{:S(2)}) %collective-permute-start.24) | collective-permute-done | bytes 32800 | tf_op jit(solution)/shard_map/ppermute | solution.py:339
  131.6 3.1 %collective-permute-start.25 = (bf16[2,128,128]{2,1,0:T(8,128)(2,1)S(1)}, bf16[2,128,128]{2,1,0:T(8,128)(2,1)S(1)}, u32[]{:S(2)}, u32[]{:S(2)}) collective-permute-start(bf16[2,128,128]{2,1,0:T(8,128)(2,1)S(1)} %get-tuple-element.46.gz), channel_id=1, source_target_pairs={{0,1},{1,2},{2,3},{3,4},{4,5},{5,6},{6,7},{7,8},{8,9},{9,10},{10,1... | collective-permute-start | bytes 196616 | tf_op jit(solution)/shard_map/ppermute | solution.py:330
  140.6 16.6 %collective-permute-start.27 = (bf16[2,64,128]{2,1,0:T(8,128)(2,1)S(1)}, bf16[2,64,128]{2,1,0:T(8,128)(2,1)S(1)}, u32[]{:S(2)}, u32[]{:S(2)}) collective-permute-start(bf16[2,64,128]{2,1,0:T(8,128)(2,1)S(1)} %get-tuple-element.48.low), channel_id=1, source_target_pairs={{240,0},{0,16},{16,32},{32,48},{48,64},{64,80},{80,96},{96,112},{1... | collective-permute-start | bytes 98312 | tf_op jit(solution)/shard_map/ppermute | solution.py:339
  158.3 5.9 %collective-permute-done.28.ahead = bf16[2,64,128]{2,1,0:T(8,128)(2,1)S(1)} collective-permute-done((bf16[2,64,128]{2,1,0:T(8,128)(2,1)S(1)}, bf16[2,64,128]{2,1,0:T(8,128)(2,1)S(1)}, u32[]{:S(2)}, u32[]{:S(2)}) %collective-permute-start.28) | collective-permute-done | bytes 32800 | tf_op jit(solution)/shard_map/ppermute | solution.py:339
  166.3 6.5 %all-to-all-start.1 = ((bf16[16,512,128]{2,1,0:T(8,128)(2,1)}), bf16[16,512,128]{2,1,0:T(8,128)(2,1)S(1)}, u32[]{:S(2)}, u32[]{:S(2)}) async-start(bf16[16,512,128]{2,1,0:T(8,128)(2,1)} %copy-done), calls=%async_computation.1 | async-start | bytes 4194304 | tf_op jit(solution)/shard_map/all_to_all | solution.py:448
  172.8 4.5 %collective-permute-start.29 = (bf16[2,128,128]{2,1,0:T(8,128)(2,1)S(1)}, bf16[2,128,128]{2,1,0:T(8,128)(2,1)S(1)}, u32[]{:S(2)}, u32[]{:S(2)}) collective-permute-start(bf16[2,128,128]{2,1,0:T(8,128)(2,1)S(1)} %get-tuple-element.52.gz), channel_id=1, source_target_pairs={{0,1},{1,2},{2,3},{3,4},{4,5},{5,6},{6,7},{7,8},{8,9},{9,10},{10,1... | collective-permute-start | bytes 196616 | tf_op jit(solution)/shard_map/ppermute | solution.py:330
  179.1 19.1 %collective-permute-done.29.left = bf16[2,128,128]{2,1,0:T(8,128)(2,1)S(1)} collective-permute-done((bf16[2,128,128]{2,1,0:T(8,128)(2,1)S(1)}, bf16[2,128,128]{2,1,0:T(8,128)(2,1)S(1)}, u32[]{:S(2)}, u32[]{:S(2)}) %collective-permute-start.29) | collective-permute-done | bytes 65568 | tf_op jit(solution)/shard_map/ppermute | solution.py:330
  201.6 16.0 %all_to_all.20.pieces = bf16[16,48,128]{2,1,0:T(8,128)(2,1)S(1)} all-to-all(bf16[16,48,128]{2,1,0:T(8,128)(2,1)S(1)} %shard_map.97), channel_id=1, replica_groups=mesh['phase'=16,'chan'=16] {'chan'}, dimensions={0} | all-to-all | bytes 393216 | tf_op jit(solution)/shard_map/all_to_all | solution.py:471
  218.3 8.7 %all-to-all-start.3 = ((bf16[16,48,128]{2,1,0:T(8,128)(2,1)}), bf16[16,48,128]{2,1,0:T(8,128)(2,1)S(1)}, u32[]{:S(2)}, u32[]{:S(2)}) async-start(bf16[16,48,128]{2,1,0:T(8,128)(2,1)} %shard_map.98), calls=%async_computation.3 | async-start | bytes 393216 | tf_op jit(solution)/shard_map/all_to_all | solution.py:473
  227.0 3.0 %collective-permute-start.31 = (bf16[1,64,128]{2,1,0:T(8,128)(2,1)S(1)}, bf16[1,64,128]{2,1,0:T(8,128)(2,1)S(1)}, u32[]{:S(2)}, u32[]{:S(2)}) collective-permute-start(bf16[1,64,128]{2,1,0:T(8,128)(2,1)S(1)} %get-tuple-element.73), channel_id=1, source_target_pairs={{240,0},{0,16},{16,32},{32,48},{48,64},{64,80},{80,96},{96,112},{1... | collective-permute-start | bytes 49160 | tf_op jit(solution)/shard_map/ppermute | solution.py:339
  230.9 5.9 %collective-permute-done.32.ahead = bf16[1,64,128]{2,1,0:T(8,128)(2,1)S(1)} collective-permute-done((bf16[1,64,128]{2,1,0:T(8,128)(2,1)S(1)}, bf16[1,64,128]{2,1,0:T(8,128)(2,1)S(1)}, u32[]{:S(2)}, u32[]{:S(2)}) %collective-permute-start.32) | collective-permute-done | bytes 16416 | tf_op jit(solution)/shard_map/ppermute | solution.py:339
  (118 shorter events, 67.6 us)
Async XLA Ops:
  3.0 32.3 %all-to-all-start = ((bf16[16,16,1728]{2,1,0:T(8,128)(2,1)}), bf16[16,16,1728]{2,1,0:T(8,128)(2,1)S(1)}, u32[]{:S(2)}, u32[]{:S(2)}) async-start(bf16[16,16,1728]{2,1,0:T(8,128)(2,1)} %broadcast_in_dim.18), calls=%async_computation | async-start | bytes 1835008 | tf_op jit(solution)/shard_map/all_to_all | solution.py:351
  35.3 29.4 %collective-permute-start = (bf16[16,16,1728]{2,1,0:T(8,128)(2,1)S(1)}, bf16[16,16,1728]{2,1,0:T(8,128)(2,1)S(1)}, u32[]{:S(2)}, u32[]{:S(2)}) collective-permute-start(bf16[16,16,1728]{2,1,0:T(8,128)(2,1)S(1)} %all-to-all-done.mine), channel_id=1, source_target_pairs={{0,16},{16,0},{32,48},{48,32},{64,80},{80,64},{96,112},{112,96},{1... | collective-permute-start | bytes 2654216 | tf_op jit(solution)/shard_map/ppermute | solution.py:373
  43.0 7.0 %collective-permute-start.3 = (bf16[2,64,128]{2,1,0:T(8,128)(2,1)S(1)}, bf16[2,64,128]{2,1,0:T(8,128)(2,1)S(1)}, u32[]{:S(2)}, u32[]{:S(2)}) collective-permute-start(bf16[2,64,128]{2,1,0:T(8,128)(2,1)S(1)} %bitcast.37), channel_id=1, source_target_pairs={{16,0},{32,16},{48,32},{64,48},{80,64},{96,80},{112,96},{128,112},... | collective-permute-start | bytes 98312 | tf_op jit(solution)/shard_map/ppermute | solution.py:339
  43.0 7.0 %collective-permute-start.4 = (bf16[1,64,128]{2,1,0:T(8,128)(2,1)S(1)}, bf16[1,64,128]{2,1,0:T(8,128)(2,1)S(1)}, u32[]{:S(2)}, u32[]{:S(2)}) collective-permute-start(bf16[1,64,128]{2,1,0:T(8,128)(2,1)S(1)} %get-tuple-element.74), channel_id=1, source_target_pairs={{32,0},{48,16},{64,32},{80,48},{96,64},{112,80},{128,96},{144,112}... | collective-permute-start | bytes 49160 | tf_op jit(solution)/shard_map/ppermute | solution.py:339
  49.9 5.8 %collective-permute-start.5 = (bf16[8,64,128]{2,1,0:T(8,128)(2,1)S(1)}, bf16[8,64,128]{2,1,0:T(8,128)(2,1)S(1)}, u32[]{:S(2)}, u32[]{:S(2)}) collective-permute-start(bf16[8,64,128]{2,1,0:T(8,128)(2,1)S(1)} %constant_dynamic-update-slice_fusion.refs_2_.own), channel_id=1, source_target_pairs={{0,2},{1,3},{2,4},{3,5},{4,6},{5,7},{6,8},{7,9},{8,10},{9,11},{10,... | collective-permute-start | bytes 393224 | tf_op jit(solution)/shard_map/ppermute | solution.py:330
  53.0 6.9 %collective-permute-start.7 = (bf16[8,64,128]{2,1,0:T(8,128)(2,1)S(1)}, bf16[8,64,128]{2,1,0:T(8,128)(2,1)S(1)}, u32[]{:S(2)}, u32[]{:S(2)}) collective-permute-start(bf16[8,64,128]{2,1,0:T(8,128)(2,1)S(1)} %constant_dynamic-update-slice_fusion.refs_2_.own), channel_id=1, source_target_pairs={{1,0},{2,1},{3,2},{4,3},{5,4},{6,5},{7,6},{8,7},{9,8},{10,9},{11,1... | collective-permute-start | bytes 393224 | tf_op jit(solution)/shard_map/ppermute | solution.py:330
  54.3 10.0 %collective-permute-start.8 = (bf16[8,64,128]{2,1,0:T(8,128)(2,1)S(1)}, bf16[8,64,128]{2,1,0:T(8,128)(2,1)S(1)}, u32[]{:S(2)}, u32[]{:S(2)}) collective-permute-start(bf16[8,64,128]{2,1,0:T(8,128)(2,1)S(1)} %constant_dynamic-update-slice_fusion.refs_2_.own), channel_id=1, source_target_pairs={{2,0},{3,1},{4,2},{5,3},{6,4},{7,5},{8,6},{9,7},{10,8},{11,9},{12,... | collective-permute-start | bytes 393224 | tf_op jit(solution)/shard_map/ppermute | solution.py:330
  67.9 6.5 %collective-permute-start.10 = (bf16[2,64,128]{2,1,0:T(8,128)(2,1)S(1)}, bf16[2,64,128]{2,1,0:T(8,128)(2,1)S(1)}, u32[]{:S(2)}, u32[]{:S(2)}) collective-permute-start(bf16[2,64,128]{2,1,0:T(8,128)(2,1)S(1)} %get-tuple-element.33.state.rest_1_), channel_id=1, source_target_pairs={{32,0},{48,16},{64,32},{80,48},{96,64},{112,80},{128,96},{144,112}... | collective-permute-start | bytes 98312 | tf_op jit(solution)/shard_map/ppermute | solution.py:339
  75.8 6.8 %collective-permute-start.12 = (bf16[2,64,128]{2,1,0:T(8,128)(2,1)S(1)}, bf16[2,64,128]{2,1,0:T(8,128)(2,1)S(1)}, u32[]{:S(2)}, u32[]{:S(2)}) collective-permute-start(bf16[2,64,128]{2,1,0:T(8,128)(2,1)S(1)} %shard_map.79.mixed.rest_1_), channel_id=1, source_target_pairs={{1,0},{2,1},{3,2},{4,3},{5,4},{6,5},{7,6},{8,7},{9,8},{10,9},{11,1... | collective-permute-start | bytes 98312 | tf_op jit(solution)/shard_map/ppermute | solution.py:330
  83.2 6.8 %collective-permute-start.14 = (bf16[2,64,128]{2,1,0:T(8,128)(2,1)S(1)}, bf16[2,64,128]{2,1,0:T(8,128)(2,1)S(1)}, u32[]{:S(2)}, u32[]{:S(2)}) collective-permute-start(bf16[2,64,128]{2,1,0:T(8,128)(2,1)S(1)} %get-tuple-element.34.state.rest_1_), channel_id=1, source_target_pairs={{64,0},{80,16},{96,32},{112,48},{128,64},{144,80},{160,96},{176,11... | collective-permute-start | bytes 98312 | tf_op jit(solution)/shard_map/ppermute | solution.py:339
  90.0 5.8 %collective-permute-start.15 = (bf16[2,64,128]{2,1,0:T(8,128)(2,1)S(1)}, bf16[2,64,128]{2,1,0:T(8,128)(2,1)S(1)}, u32[]{:S(2)}, u32[]{:S(2)}) collective-permute-start(bf16[2,64,128]{2,1,0:T(8,128)(2,1)S(1)} %shard_map.81.mixed.rest_1_), channel_id=1, source_target_pairs={{0,1},{1,2},{2,3},{3,4},{4,5},{5,6},{6,7},{7,8},{8,9},{9,10},{10,1... | collective-permute-start | bytes 98312 | tf_op jit(solution)/shard_map/ppermute | solution.py:330
  99.5 5.5 %collective-permute-start.17 = (bf16[2,128,128]{2,1,0:T(8,128)(2,1)S(1)}, bf16[2,128,128]{2,1,0:T(8,128)(2,1)S(1)}, u32[]{:S(2)}, u32[]{:S(2)}) collective-permute-start(bf16[2,128,128]{2,1,0:T(8,128)(2,1)S(1)} %get-tuple-element.36.gz), channel_id=1, source_target_pairs={{0,1},{1,2},{2,3},{3,4},{4,5},{5,6},{6,7},{7,8},{8,9},{9,10},{10,1... | collective-permute-start | bytes 196616 | tf_op jit(solution)/shard_map/ppermute | solution.py:330
  108.7 6.7 %collective-permute-start.20 = (bf16[2,64,128]{2,1,0:T(8,128)(2,1)S(1)}, bf16[2,64,128]{2,1,0:T(8,128)(2,1)S(1)}, u32[]{:S(2)}, u32[]{:S(2)}) collective-permute-start(bf16[2,64,128]{2,1,0:T(8,128)(2,1)S(1)} %get-tuple-element.37.low), channel_id=1, source_target_pairs={{64,0},{80,16},{96,32},{112,48},{128,64},{144,80},{160,96},{176,11... | collective-permute-start | bytes 98312 | tf_op jit(solution)/shard_map/ppermute | solution.py:339
  117.9 5.1 %collective-permute-start.22 = (bf16[2,128,128]{2,1,0:T(8,128)(2,1)S(1)}, bf16[2,128,128]{2,1,0:T(8,128)(2,1)S(1)}, u32[]{:S(2)}, u32[]{:S(2)}) collective-permute-start(bf16[2,128,128]{2,1,0:T(8,128)(2,1)S(1)} %get-tuple-element.41.gz), channel_id=1, source_target_pairs={{1,0},{2,1},{3,2},{4,3},{5,4},{6,5},{7,6},{8,7},{9,8},{10,9},{11,1... | collective-permute-start | bytes 196616 | tf_op jit(solution)/shard_map/ppermute | solution.py:330
  125.1 6.4 %collective-permute-start.24 = (bf16[2,64,128]{2,1,0:T(8,128)(2,1)S(1)}, bf16[2,64,128]{2,1,0:T(8,128)(2,1)S(1)}, u32[]{:S(2)}, u32[]{:S(2)}) collective-permute-start(bf16[2,64,128]{2,1,0:T(8,128)(2,1)S(1)} %get-tuple-element.42.low), channel_id=1, source_target_pairs={{32,0},{48,16},{64,32},{80,48},{96,64},{112,80},{128,96},{144,112}... | collective-permute-start | bytes 98312 | tf_op jit(solution)/shard_map/ppermute | solution.py:339
  131.6 7.5 %collective-permute-start.25 = (bf16[2,128,128]{2,1,0:T(8,128)(2,1)S(1)}, bf16[2,128,128]{2,1,0:T(8,128)(2,1)S(1)}, u32[]{:S(2)}, u32[]{:S(2)}) collective-permute-start(bf16[2,128,128]{2,1,0:T(8,128)(2,1)S(1)} %get-tuple-element.46.gz), channel_id=1, source_target_pairs={{0,1},{1,2},{2,3},{3,4},{4,5},{5,6},{6,7},{7,8},{8,9},{9,10},{10,1... | collective-permute-start | bytes 196616 | tf_op jit(solution)/shard_map/ppermute | solution.py:330
  134.7 5.1 %collective-permute-start.26 = (bf16[2,128,128]{2,1,0:T(8,128)(2,1)S(1)}, bf16[2,128,128]{2,1,0:T(8,128)(2,1)S(1)}, u32[]{:S(2)}, u32[]{:S(2)}) collective-permute-start(bf16[2,128,128]{2,1,0:T(8,128)(2,1)S(1)} %get-tuple-element.46.gz), channel_id=1, source_target_pairs={{1,0},{2,1},{3,2},{4,3},{5,4},{6,5},{7,6},{8,7},{9,8},{10,9},{11,1... | collective-permute-start | bytes 196616 | tf_op jit(solution)/shard_map/ppermute | solution.py:330
  140.6 17.7 %collective-permute-start.27 = (bf16[2,64,128]{2,1,0:T(8,128)(2,1)S(1)}, bf16[2,64,128]{2,1,0:T(8,128)(2,1)S(1)}, u32[]{:S(2)}, u32[]{:S(2)}) collective-permute-start(bf16[2,64,128]{2,1,0:T(8,128)(2,1)S(1)} %get-tuple-element.48.low), channel_id=1, source_target_pairs={{240,0},{0,16},{16,32},{32,48},{48,64},{64,80},{80,96},{96,112},{1... | collective-permute-start | bytes 98312 | tf_op jit(solution)/shard_map/ppermute | solution.py:339
  157.2 7.0 %collective-permute-start.28 = (bf16[2,64,128]{2,1,0:T(8,128)(2,1)S(1)}, bf16[2,64,128]{2,1,0:T(8,128)(2,1)S(1)}, u32[]{:S(2)}, u32[]{:S(2)}) collective-permute-start(bf16[2,64,128]{2,1,0:T(8,128)(2,1)S(1)} %get-tuple-element.48.low), channel_id=1, source_target_pairs={{16,0},{32,16},{48,32},{64,48},{80,64},{96,80},{112,96},{128,112},... | collective-permute-start | bytes 98312 | tf_op jit(solution)/shard_map/ppermute | solution.py:339
  166.3 34.9 %all-to-all-start.1 = ((bf16[16,512,128]{2,1,0:T(8,128)(2,1)}), bf16[16,512,128]{2,1,0:T(8,128)(2,1)S(1)}, u32[]{:S(2)}, u32[]{:S(2)}) async-start(bf16[16,512,128]{2,1,0:T(8,128)(2,1)} %copy-done), calls=%async_computation.1 | async-start | bytes 4194304 | tf_op jit(solution)/shard_map/all_to_all | solution.py:448
  172.8 25.4 %collective-permute-start.29 = (bf16[2,128,128]{2,1,0:T(8,128)(2,1)S(1)}, bf16[2,128,128]{2,1,0:T(8,128)(2,1)S(1)}, u32[]{:S(2)}, u32[]{:S(2)}) collective-permute-start(bf16[2,128,128]{2,1,0:T(8,128)(2,1)S(1)} %get-tuple-element.52.gz), channel_id=1, source_target_pairs={{0,1},{1,2},{2,3},{3,4},{4,5},{5,6},{6,7},{7,8},{8,9},{9,10},{10,1... | collective-permute-start | bytes 196616 | tf_op jit(solution)/shard_map/ppermute | solution.py:330
  177.3 22.8 %collective-permute-start.30 = (bf16[2,128,128]{2,1,0:T(8,128)(2,1)S(1)}, bf16[2,128,128]{2,1,0:T(8,128)(2,1)S(1)}, u32[]{:S(2)}, u32[]{:S(2)}) collective-permute-start(bf16[2,128,128]{2,1,0:T(8,128)(2,1)S(1)} %get-tuple-element.52.gz), channel_id=1, source_target_pairs={{1,0},{2,1},{3,2},{4,3},{5,4},{6,5},{7,6},{8,7},{9,8},{10,9},{11,1... | collective-permute-start | bytes 196616 | tf_op jit(solution)/shard_map/ppermute | solution.py:330
  218.3 19.3 %all-to-all-start.3 = ((bf16[16,48,128]{2,1,0:T(8,128)(2,1)}), bf16[16,48,128]{2,1,0:T(8,128)(2,1)S(1)}, u32[]{:S(2)}, u32[]{:S(2)}) async-start(bf16[16,48,128]{2,1,0:T(8,128)(2,1)} %shard_map.98), calls=%async_computation.3 | async-start | bytes 393216 | tf_op jit(solution)/shard_map/all_to_all | solution.py:473
  230.0 6.8 %collective-permute-start.32 = (bf16[1,64,128]{2,1,0:T(8,128)(2,1)S(1)}, bf16[1,64,128]{2,1,0:T(8,128)(2,1)S(1)}, u32[]{:S(2)}, u32[]{:S(2)}) collective-permute-start(bf16[1,64,128]{2,1,0:T(8,128)(2,1)S(1)} %get-tuple-element.72), channel_id=1, source_target_pairs={{16,0},{32,16},{48,32},{64,48},{80,64},{96,80},{112,96},{128,112},... | collective-permute-start | bytes 49160 | tf_op jit(solution)/shard_map/ppermute | solution.py:339
  (16 other events, 141.8 us)

commit v3 on v2

--- a/solution.py
+++ b/solution.py
@@ -231,16 +231,7 @@
         tap[:, which : which + 1] = jnp.sum(totals[which], axis=1, keepdims=True)
 
 
-def weight_kernel(offsets, gz, *rest):
-    sources, (out, columns) = rest[:-2], rest[-2:]
-    if len(sources) == 2:
-        sources, held = sources[:1], sources[1]
-        out[:, 128:] = held[...]
-    if len(sources) == 1:
-        x, t = offsets
-        planes = [[sources[0][x + n, t], sources[0][x + n, t + 1]] for n in range(3)]
-    else:
-        planes = [[a[0], a[1]] for a in sources]
+def weight_product(gz, planes, columns):
     fill_columns(columns, planes, 1)
     both = jnp.concatenate([gz[0], gz[1]], axis=1)
     order = permutation(lambda r: r % 8 // 4 * 64 + r // 8 * 4 + r % 4)
@@ -248,15 +239,45 @@
     grad = lax.dot_general(
         columns[...], both, (((1,), (1,)), ((), ())), preferred_element_type=f32
     )
-    out[:13, :128] = grad[: 13 * 128].astype(bf16).reshape(13, 128, 128)
-    out[13, :CHANS] = grad[13 * 128 :].astype(bf16)
-    out[13, CHANS:128] = jnp.zeros((CHANS, 128), bf16)
-    out[14:, :128] = jnp.zeros((2, 128, 128), bf16)
+    grad = grad.astype(bf16)
+    pieces = [grad[n * 128 : (n + 1) * 128] for n in range(13)]
+    pieces.append(jnp.concatenate([grad[13 * 128 :], jnp.zeros((CHANS, 128), bf16)], axis=0))
+    return pieces + [jnp.zeros((128, 128), bf16)] * 2
+
+
+def weight_kernel(offsets, gz, *rest):
+    sources, (out, columns) = rest[:-2], rest[-2:]
+    if len(sources) == 1:
+        x, t = offsets
+        planes = [[sources[0][x + n, t], sources[0][x + n, t + 1]] for n in range(3)]
+    else:
+        planes = [[a[0], a[1]] for a in sources]
+    for n, piece in enumerate(weight_product(gz, planes, columns)):
+        out[n] = piece
+
+
+def last_weight_kernel(offsets, odd, gz, mixed, held3, held2, held1, keep, send, columns):
+    x, t = offsets
+    planes = [[mixed[x + n, t], mixed[x + n, t + 1]] for n in range(3)]
+    pieces = weight_product(gz, planes, columns)
+    mine = odd[:1, :1] > 0.5
+    for m in range(8):
+        pairs = [(pieces[2 * m], pieces[2 * m + 1])]
+        pairs += [(held[2 * m], held[2 * m + 1]) for held in (held1, held2, held3)]
+        for b, (even_part, odd_part) in enumerate(pairs):
+            lower, upper = even_part.astype(f32), odd_part.astype(f32)
+            rows = slice(128 * b, 128 * b + 128)
+            keep[m, rows] = jnp.where(mine, upper, lower).astype(bf16)
+            send[m, rows] = jnp.where(mine, lower, upper).astype(bf16)
+
+
+def join_kernel(keep, other, out):
+    out[...] = (keep[...].astype(f32) + other[...].astype(f32)).astype(bf16)
 
 
 def turned_sum(pieces, start):
     total = pieces[0, start : start + 128].astype(f32)
-    for n in range(1, 16):
+    for n in range(1, 8):
         total = total + pieces[n, start : start + 128].astype(f32)
     r = lax.broadcasted_iota(jnp.int32, (128, 128), 0)
     c = lax.broadcasted_iota(jnp.int32, (128, 128), 1)
@@ -274,7 +295,7 @@
 
 
 def pack_kernel(pieces, taps, out):
-    parts = [turned_sum(pieces, start) for start in (0, 384, 256, 128)]
+    parts = [turned_sum(pieces, 128 * b) for b in range(BLOCKS)]
     high, low = halves(taps[...])
     for j in range(16):
         for b in range(BLOCKS):
@@ -436,16 +457,29 @@
     for b in reversed(range(BLOCKS)):
         line, mixed, offsets, _, _ = saved[b]
         gleft, gright = sides(gz, "chan")
-        extra = [jnp.concatenate(held, axis=1)] if b == 0 else []
-        pieces = call(
-            functools.partial(weight_kernel, offsets),
-            shaped((16, 128 + 384 * len(extra), 128), bf16),
-            gz, *mixed, *extra,
-            scratch=[columns],
-        )
-        held.append(pieces)
+        if b > 0:
+            pieces = call(
+                functools.partial(weight_kernel, offsets),
+                shaped((16, 128, 128), bf16),
+                gz, *mixed,
+                scratch=[columns],
+            )
+            held.append(pieces)
+        else:
+            keep, send = call(
+                functools.partial(last_weight_kernel, offsets),
+                [shaped((8, 512, 128), bf16)] * 2,
+                odd, gz, *mixed, *held,
+                scratch=[columns],
+                room=16,
+            )
         if b == 0:
-            late = lax.all_to_all(pieces, "phase", 0, 0, tiled=True)
+            other = lax.ppermute(send, "phase", [(i, i ^ 1) for i in range(count)])
+            late = call(join_kernel, shaped((8, 512, 128), bf16), keep, other)
+            alike = [list(range(n, count, 2)) for n in range(2)]
+            late = lax.all_to_all(
+                late, "phase", 0, 0, tiled=True, axis_index_groups=alike
+            )
         low, tap_grads[b] = call(
             functools.partial(data_kernel, b),
             [shaped(unit, bf16), shaped((CHANS, 3), f32)],

time: 240 us -> 232 us (0.967)
  waiting for transfers between devices: 106 us -> 97.6 us
    ppermute x16, waiting for transfers between devices: 44.6 us -> 35.2 us  [beside(): return lax.ppermute(cells, axis, pairs)]
    ppermute x0 -> x1, waiting for transfers between devices: none -> 2.65 us  [per_device(): other = lax.ppermute(send, 'phase', [(i, i ^ 1) for i in range(count)])]
    pallas_call x24 -> x25, Pallas kernels: 14.9 us -> 16.2 us  [call(): pl.pallas_call(body, out_shape=out_shape, scratch_shapes=list(scratch), c...]
  transfers between devices with their start and end apart: 36 -> 37, of which waited for: 24 -> 24; matrix products, arithmetic and copies ran while one was open for 1% -> 1% of each run, Pallas kernels for 3% -> 3%
where the time goes in v3:
time: 232 us; the launch traced here: 231 us
  waiting for transfers between devices  97.6 us (42%)
  starting transfers between devices  94.9 us (41%)
  Pallas kernels  16.2 us (7%)
  blocking collectives  15.4 us (7%)
  local copies, waits for them, and re-layouts  5.07 us (2%)
    ppermute x16, waiting for transfers between devices, turned(): lax.ppermute(block, 'phase', [((i - distance) % count, i) for i in range(...  36.8 us
    ppermute x16, waiting for transfers between devices, beside(): return lax.ppermute(cells, axis, pairs)  35.2 us
    ppermute x16, starting transfers between devices, turned(): lax.ppermute(block, 'phase', [((i - distance) % count, i) for i in range(...  33.4 us
    ppermute x16, starting transfers between devices, beside(): return lax.ppermute(cells, axis, pairs)  32.3 us
    all_to_all x1, waiting for transfers between devices, spread(): return lax.all_to_all(copies, axis, 0, 0, tiled=True)  23 us
    pallas_call x25, Pallas kernels, call(): pl.pallas_call(body, out_shape=out_shape, scratch_shapes=list(scratch), c...  16.2 us
    all_to_all x1, blocking collectives, per_device(): packed = lax.all_to_all(packed, 'chan', 0, 0, tiled=True)  15.4 us
    all_to_all x1, starting transfers between devices, per_device(): packed = lax.all_to_all(packed, 'phase', 0, 0, tiled=True)  9.7 us
  transfers between devices with their start and end apart: 37, of which 24 were waited for; matrix products, arithmetic and copies ran while one was open for 1% of the time, Pallas kernels for 3%

profile of v3, /device:TPU:7, one launch (start us, length us, event | category | flops | bytes accessed | tf_op | source)
XLA Modules:
  0.0 231.4 jit_solution(1850440077547704001)
XLA Ops:
  2.9 9.4 %all-to-all-start = ((bf16[16,16,1728]{2,1,0:T(8,128)(2,1)}), bf16[16,16,1728]{2,1,0:T(8,128)(2,1)S(1)}, u32[]{:S(2)}, u32[]{:S(2)}) async-start(bf16[16,16,1728]{2,1,0:T(8,128)(2,1)} %broadcast_in_dim.18), calls=%async_computation | async-start | bytes 1835008 | tf_op jit(solution)/shard_map/all_to_all | solution.py:372
  12.4 23.0 %all-to-all-done.mine = bf16[16,16,1728]{2,1,0:T(8,128)(2,1)S(1)} async-done(((bf16[16,16,1728]{2,1,0:T(8,128)(2,1)}), bf16[16,16,1728]{2,1,0:T(8,128)(2,1)S(1)}, u32[]{:S(2)}, u32[]{:S(2)}) %all-to-all-start) | async-done | bytes 884768 | tf_op jit(solution)/shard_map/all_to_all | solution.py:372
  35.4 3.8 %collective-permute-start = (bf16[16,16,1728]{2,1,0:T(8,128)(2,1)S(1)}, bf16[16,16,1728]{2,1,0:T(8,128)(2,1)S(1)}, u32[]{:S(2)}, u32[]{:S(2)}) collective-permute-start(bf16[16,16,1728]{2,1,0:T(8,128)(2,1)S(1)} %all-to-all-done.mine), channel_id=1, source_target_pairs={{0,16},{16,0},{32,48},{48,32},{64,80},{80,64},{96,112},{112,96},{1... | collective-permute-start | bytes 2654216 | tf_op jit(solution)/shard_map/ppermute | solution.py:394
  44.1 5.9 %collective-permute-done.3 = bf16[2,64,128]{2,1,0:T(8,128)(2,1)S(1)} collective-permute-done((bf16[2,64,128]{2,1,0:T(8,128)(2,1)S(1)}, bf16[2,64,128]{2,1,0:T(8,128)(2,1)S(1)}, u32[]{:S(2)}, u32[]{:S(2)}) %collective-permute-start.3) | collective-permute-done | bytes 32800 | tf_op jit(solution)/shard_map/ppermute | solution.py:360
  55.9 4.1 %collective-permute-done.7.refs_3_.after_own = bf16[8,64,128]{2,1,0:T(8,128)(2,1)S(1)} collective-permute-done((bf16[8,64,128]{2,1,0:T(8,128)(2,1)S(1)}, bf16[8,64,128]{2,1,0:T(8,128)(2,1)S(1)}, u32[]{:S(2)}, u32[]{:S(2)}) %collective-permute-start.7) | collective-permute-done | bytes 131104 | tf_op jit(solution)/shard_map/ppermute | solution.py:351
  60.0 4.3 %collective-permute-done.8.refs_4_ = bf16[8,64,128]{2,1,0:T(8,128)(2,1)S(1)} collective-permute-done((bf16[8,64,128]{2,1,0:T(8,128)(2,1)S(1)}, bf16[8,64,128]{2,1,0:T(8,128)(2,1)S(1)}, u32[]{:S(2)}, u32[]{:S(2)}) %collective-permute-start.8) | collective-permute-done | bytes 131104 | tf_op jit(solution)/shard_map/ppermute | solution.py:351
  70.6 3.7 %collective-permute-done.10.ahead.rest_2_ = bf16[2,64,128]{2,1,0:T(8,128)(2,1)S(1)} collective-permute-done((bf16[2,64,128]{2,1,0:T(8,128)(2,1)S(1)}, bf16[2,64,128]{2,1,0:T(8,128)(2,1)S(1)}, u32[]{:S(2)}, u32[]{:S(2)}) %collective-permute-start.10) | collective-permute-done | bytes 32800 | tf_op jit(solution)/shard_map/ppermute | solution.py:360
  77.6 5.1 %collective-permute-done.12.right.rest_2_ = bf16[2,64,128]{2,1,0:T(8,128)(2,1)S(1)} collective-permute-done((bf16[2,64,128]{2,1,0:T(8,128)(2,1)S(1)}, bf16[2,64,128]{2,1,0:T(8,128)(2,1)S(1)}, u32[]{:S(2)}, u32[]{:S(2)}) %collective-permute-start.12) | collective-permute-done | bytes 32800 | tf_op jit(solution)/shard_map/ppermute | solution.py:351
  83.3 3.0 %collective-permute-start.14 = (bf16[2,64,128]{2,1,0:T(8,128)(2,1)S(1)}, bf16[2,64,128]{2,1,0:T(8,128)(2,1)S(1)}, u32[]{:S(2)}, u32[]{:S(2)}) collective-permute-start(bf16[2,64,128]{2,1,0:T(8,128)(2,1)S(1)} %get-tuple-element.36.state.rest_1_), channel_id=1, source_target_pairs={{64,0},{80,16},{96,32},{112,48},{128,64},{144,80},{160,96},{176,11... | collective-permute-start | bytes 98312 | tf_op jit(solution)/shard_map/ppermute | solution.py:360
  90.2 4.3 %collective-permute-start.15 = (bf16[2,64,128]{2,1,0:T(8,128)(2,1)S(1)}, bf16[2,64,128]{2,1,0:T(8,128)(2,1)S(1)}, u32[]{:S(2)}, u32[]{:S(2)}) collective-permute-start(bf16[2,64,128]{2,1,0:T(8,128)(2,1)S(1)} %shard_map.81.mixed.rest_1_), channel_id=1, source_target_pairs={{0,1},{1,2},{2,3},{3,4},{4,5},{5,6},{6,7},{7,8},{8,9},{9,10},{10,1... | collective-permute-start | bytes 98312 | tf_op jit(solution)/shard_map/ppermute | solution.py:351
  96.0 3.1 %collective-permute-done.16.right.rest_2_ = bf16[2,64,128]{2,1,0:T(8,128)(2,1)S(1)} collective-permute-done((bf16[2,64,128]{2,1,0:T(8,128)(2,1)S(1)}, bf16[2,64,128]{2,1,0:T(8,128)(2,1)S(1)}, u32[]{:S(2)}, u32[]{:S(2)}) %collective-permute-start.16) | collective-permute-done | bytes 32800 | tf_op jit(solution)/shard_map/ppermute | solution.py:351
  112.6 2.9 %collective-permute-done.20.ahead = bf16[2,64,128]{2,1,0:T(8,128)(2,1)S(1)} collective-permute-done((bf16[2,64,128]{2,1,0:T(8,128)(2,1)S(1)}, bf16[2,64,128]{2,1,0:T(8,128)(2,1)S(1)}, u32[]{:S(2)}, u32[]{:S(2)}) %collective-permute-start.20) | collective-permute-done | bytes 32800 | tf_op jit(solution)/shard_map/ppermute | solution.py:360
  119.5 3.8 %collective-permute-done.22.right = bf16[2,128,128]{2,1,0:T(8,128)(2,1)S(1)} collective-permute-done((bf16[2,128,128]{2,1,0:T(8,128)(2,1)S(1)}, bf16[2,128,128]{2,1,0:T(8,128)(2,1)S(1)}, u32[]{:S(2)}, u32[]{:S(2)}) %collective-permute-start.22) | collective-permute-done | bytes 65568 | tf_op jit(solution)/shard_map/ppermute | solution.py:351
  126.9 4.8 %collective-permute-done.24.ahead = bf16[2,64,128]{2,1,0:T(8,128)(2,1)S(1)} collective-permute-done((bf16[2,64,128]{2,1,0:T(8,128)(2,1)S(1)}, bf16[2,64,128]{2,1,0:T(8,128)(2,1)S(1)}, u32[]{:S(2)}, u32[]{:S(2)}) %collective-permute-start.24) | collective-permute-done | bytes 32800 | tf_op jit(solution)/shard_map/ppermute | solution.py:360
  131.9 3.1 %collective-permute-start.25 = (bf16[2,128,128]{2,1,0:T(8,128)(2,1)S(1)}, bf16[2,128,128]{2,1,0:T(8,128)(2,1)S(1)}, u32[]{:S(2)}, u32[]{:S(2)}) collective-permute-start(bf16[2,128,128]{2,1,0:T(8,128)(2,1)S(1)} %get-tuple-element.48.gz), channel_id=1, source_target_pairs={{0,1},{1,2},{2,3},{3,4},{4,5},{5,6},{6,7},{7,8},{8,9},{9,10},{10,1... | collective-permute-start | bytes 196616 | tf_op jit(solution)/shard_map/ppermute | solution.py:351
  140.9 16.6 %collective-permute-start.27 = (bf16[2,64,128]{2,1,0:T(8,128)(2,1)S(1)}, bf16[2,64,128]{2,1,0:T(8,128)(2,1)S(1)}, u32[]{:S(2)}, u32[]{:S(2)}) collective-permute-start(bf16[2,64,128]{2,1,0:T(8,128)(2,1)S(1)} %get-tuple-element.50.low), channel_id=1, source_target_pairs={{240,0},{0,16},{16,32},{32,48},{48,64},{64,80},{80,96},{96,112},{1... | collective-permute-start | bytes 98312 | tf_op jit(solution)/shard_map/ppermute | solution.py:360
  159.6 4.8 %collective-permute-done.28.ahead = bf16[2,64,128]{2,1,0:T(8,128)(2,1)S(1)} collective-permute-done((bf16[2,64,128]{2,1,0:T(8,128)(2,1)S(1)}, bf16[2,64,128]{2,1,0:T(8,128)(2,1)S(1)}, u32[]{:S(2)}, u32[]{:S(2)}) %collective-permute-start.28) | collective-permute-done | bytes 32800 | tf_op jit(solution)/shard_map/ppermute | solution.py:360
  169.5 6.2 %all-to-all-start.1 = ((bf16[8,512,128]{2,1,0:T(8,128)(2,1)}), bf16[8,512,128]{2,1,0:T(8,128)(2,1)S(1)}, u32[]{:S(2)}, u32[]{:S(2)}) async-start(bf16[8,512,128]{2,1,0:T(8,128)(2,1)} %shard_map.97), calls=%async_computation.1 | async-start | bytes 2097152 | tf_op jit(solution)/shard_map/all_to_all | solution.py:480
  175.7 4.5 %collective-permute-start.29 = (bf16[2,128,128]{2,1,0:T(8,128)(2,1)S(1)}, bf16[2,128,128]{2,1,0:T(8,128)(2,1)S(1)}, u32[]{:S(2)}, u32[]{:S(2)}) collective-permute-start(bf16[2,128,128]{2,1,0:T(8,128)(2,1)S(1)} %get-tuple-element.54.gz), channel_id=1, source_target_pairs={{0,1},{1,2},{2,3},{3,4},{4,5},{5,6},{6,7},{7,8},{8,9},{9,10},{10,1... | collective-permute-start | bytes 196616 | tf_op jit(solution)/shard_map/ppermute | solution.py:351
  181.9 8.1 %collective-permute-done.29.left = bf16[2,128,128]{2,1,0:T(8,128)(2,1)S(1)} collective-permute-done((bf16[2,128,128]{2,1,0:T(8,128)(2,1)S(1)}, bf16[2,128,128]{2,1,0:T(8,128)(2,1)S(1)}, u32[]{:S(2)}, u32[]{:S(2)}) %collective-permute-start.29) | collective-permute-done | bytes 65568 | tf_op jit(solution)/shard_map/ppermute | solution.py:351
  193.2 15.4 %all_to_all.20.pieces = bf16[16,48,128]{2,1,0:T(8,128)(2,1)S(1)} all-to-all(bf16[16,48,128]{2,1,0:T(8,128)(2,1)S(1)} %shard_map.98), channel_id=1, replica_groups=mesh['phase'=16,'chan'=16] {'chan'}, dimensions={0} | all-to-all | bytes 393216 | tf_op jit(solution)/shard_map/all_to_all | solution.py:505
  209.4 9.7 %all-to-all-start.3 = ((bf16[16,48,128]{2,1,0:T(8,128)(2,1)}), bf16[16,48,128]{2,1,0:T(8,128)(2,1)S(1)}, u32[]{:S(2)}, u32[]{:S(2)}) async-start(bf16[16,48,128]{2,1,0:T(8,128)(2,1)} %shard_map.99), calls=%async_computation.3 | async-start | bytes 393216 | tf_op jit(solution)/shard_map/all_to_all | solution.py:507
  219.1 3.0 %collective-permute-start.31 = (bf16[1,64,128]{2,1,0:T(8,128)(2,1)S(1)}, bf16[1,64,128]{2,1,0:T(8,128)(2,1)S(1)}, u32[]{:S(2)}, u32[]{:S(2)}) collective-permute-start(bf16[1,64,128]{2,1,0:T(8,128)(2,1)S(1)} %get-tuple-element.77), channel_id=1, source_target_pairs={{240,0},{0,16},{16,32},{32,48},{48,64},{64,80},{80,96},{96,112},{1... | collective-permute-start | bytes 49160 | tf_op jit(solution)/shard_map/ppermute | solution.py:360
  223.0 5.9 %collective-permute-done.32.ahead = bf16[1,64,128]{2,1,0:T(8,128)(2,1)S(1)} collective-permute-done((bf16[1,64,128]{2,1,0:T(8,128)(2,1)S(1)}, bf16[1,64,128]{2,1,0:T(8,128)(2,1)S(1)}, u32[]{:S(2)}, u32[]{:S(2)}) %collective-permute-start.32) | collective-permute-done | bytes 16416 | tf_op jit(solution)/shard_map/ppermute | solution.py:360
  (118 shorter events, 71.5 us)
Async XLA Ops:
  2.9 32.5 %all-to-all-start = ((bf16[16,16,1728]{2,1,0:T(8,128)(2,1)}), bf16[16,16,1728]{2,1,0:T(8,128)(2,1)S(1)}, u32[]{:S(2)}, u32[]{:S(2)}) async-start(bf16[16,16,1728]{2,1,0:T(8,128)(2,1)} %broadcast_in_dim.18), calls=%async_computation | async-start | bytes 1835008 | tf_op jit(solution)/shard_map/all_to_all | solution.py:372
  35.4 29.3 %collective-permute-start = (bf16[16,16,1728]{2,1,0:T(8,128)(2,1)S(1)}, bf16[16,16,1728]{2,1,0:T(8,128)(2,1)S(1)}, u32[]{:S(2)}, u32[]{:S(2)}) collective-permute-start(bf16[16,16,1728]{2,1,0:T(8,128)(2,1)S(1)} %all-to-all-done.mine), channel_id=1, source_target_pairs={{0,16},{16,0},{32,48},{48,32},{64,80},{80,64},{96,112},{112,96},{1... | collective-permute-start | bytes 2654216 | tf_op jit(solution)/shard_map/ppermute | solution.py:394
  43.1 7.0 %collective-permute-start.3 = (bf16[2,64,128]{2,1,0:T(8,128)(2,1)S(1)}, bf16[2,64,128]{2,1,0:T(8,128)(2,1)S(1)}, u32[]{:S(2)}, u32[]{:S(2)}) collective-permute-start(bf16[2,64,128]{2,1,0:T(8,128)(2,1)S(1)} %bitcast.37), channel_id=1, source_target_pairs={{16,0},{32,16},{48,32},{64,48},{80,64},{96,80},{112,96},{128,112},... | collective-permute-start | bytes 98312 | tf_op jit(solution)/shard_map/ppermute | solution.py:360
  43.1 7.0 %collective-permute-start.4 = (bf16[1,64,128]{2,1,0:T(8,128)(2,1)S(1)}, bf16[1,64,128]{2,1,0:T(8,128)(2,1)S(1)}, u32[]{:S(2)}, u32[]{:S(2)}) collective-permute-start(bf16[1,64,128]{2,1,0:T(8,128)(2,1)S(1)} %get-tuple-element.78), channel_id=1, source_target_pairs={{32,0},{48,16},{64,32},{80,48},{96,64},{112,80},{128,96},{144,112}... | collective-permute-start | bytes 49160 | tf_op jit(solution)/shard_map/ppermute | solution.py:360
  50.1 5.8 %collective-permute-start.5 = (bf16[8,64,128]{2,1,0:T(8,128)(2,1)S(1)}, bf16[8,64,128]{2,1,0:T(8,128)(2,1)S(1)}, u32[]{:S(2)}, u32[]{:S(2)}) collective-permute-start(bf16[8,64,128]{2,1,0:T(8,128)(2,1)S(1)} %constant_dynamic-update-slice_fusion.refs_2_.own), channel_id=1, source_target_pairs={{0,2},{1,3},{2,4},{3,5},{4,6},{5,7},{6,8},{7,9},{8,10},{9,11},{10,... | collective-permute-start | bytes 393224 | tf_op jit(solution)/shard_map/ppermute | solution.py:351
  53.1 6.9 %collective-permute-start.7 = (bf16[8,64,128]{2,1,0:T(8,128)(2,1)S(1)}, bf16[8,64,128]{2,1,0:T(8,128)(2,1)S(1)}, u32[]{:S(2)}, u32[]{:S(2)}) collective-permute-start(bf16[8,64,128]{2,1,0:T(8,128)(2,1)S(1)} %constant_dynamic-update-slice_fusion.refs_2_.own), channel_id=1, source_target_pairs={{1,0},{2,1},{3,2},{4,3},{5,4},{6,5},{7,6},{8,7},{9,8},{10,9},{11,1... | collective-permute-start | bytes 393224 | tf_op jit(solution)/shard_map/ppermute | solution.py:351
  54.4 9.9 %collective-permute-start.8 = (bf16[8,64,128]{2,1,0:T(8,128)(2,1)S(1)}, bf16[8,64,128]{2,1,0:T(8,128)(2,1)S(1)}, u32[]{:S(2)}, u32[]{:S(2)}) collective-permute-start(bf16[8,64,128]{2,1,0:T(8,128)(2,1)S(1)} %constant_dynamic-update-slice_fusion.refs_2_.own), channel_id=1, source_target_pairs={{2,0},{3,1},{4,2},{5,3},{6,4},{7,5},{8,6},{9,7},{10,8},{11,9},{12,... | collective-permute-start | bytes 393224 | tf_op jit(solution)/shard_map/ppermute | solution.py:351
  67.9 6.5 %collective-permute-start.10 = (bf16[2,64,128]{2,1,0:T(8,128)(2,1)S(1)}, bf16[2,64,128]{2,1,0:T(8,128)(2,1)S(1)}, u32[]{:S(2)}, u32[]{:S(2)}) collective-permute-start(bf16[2,64,128]{2,1,0:T(8,128)(2,1)S(1)} %get-tuple-element.35.state.rest_1_), channel_id=1, source_target_pairs={{32,0},{48,16},{64,32},{80,48},{96,64},{112,80},{128,96},{144,112}... | collective-permute-start | bytes 98312 | tf_op jit(solution)/shard_map/ppermute | solution.py:360
  75.8 7.0 %collective-permute-start.12 = (bf16[2,64,128]{2,1,0:T(8,128)(2,1)S(1)}, bf16[2,64,128]{2,1,0:T(8,128)(2,1)S(1)}, u32[]{:S(2)}, u32[]{:S(2)}) collective-permute-start(bf16[2,64,128]{2,1,0:T(8,128)(2,1)S(1)} %shard_map.79.mixed.rest_1_), channel_id=1, source_target_pairs={{1,0},{2,1},{3,2},{4,3},{5,4},{6,5},{7,6},{8,7},{9,8},{10,9},{11,1... | collective-permute-start | bytes 98312 | tf_op jit(solution)/shard_map/ppermute | solution.py:351
  83.3 6.8 %collective-permute-start.14 = (bf16[2,64,128]{2,1,0:T(8,128)(2,1)S(1)}, bf16[2,64,128]{2,1,0:T(8,128)(2,1)S(1)}, u32[]{:S(2)}, u32[]{:S(2)}) collective-permute-start(bf16[2,64,128]{2,1,0:T(8,128)(2,1)S(1)} %get-tuple-element.36.state.rest_1_), channel_id=1, source_target_pairs={{64,0},{80,16},{96,32},{112,48},{128,64},{144,80},{160,96},{176,11... | collective-permute-start | bytes 98312 | tf_op jit(solution)/shard_map/ppermute | solution.py:360
  90.2 5.8 %collective-permute-start.15 = (bf16[2,64,128]{2,1,0:T(8,128)(2,1)S(1)}, bf16[2,64,128]{2,1,0:T(8,128)(2,1)S(1)}, u32[]{:S(2)}, u32[]{:S(2)}) collective-permute-start(bf16[2,64,128]{2,1,0:T(8,128)(2,1)S(1)} %shard_map.81.mixed.rest_1_), channel_id=1, source_target_pairs={{0,1},{1,2},{2,3},{3,4},{4,5},{5,6},{6,7},{7,8},{8,9},{9,10},{10,1... | collective-permute-start | bytes 98312 | tf_op jit(solution)/shard_map/ppermute | solution.py:351
  99.6 5.5 %collective-permute-start.17 = (bf16[2,128,128]{2,1,0:T(8,128)(2,1)S(1)}, bf16[2,128,128]{2,1,0:T(8,128)(2,1)S(1)}, u32[]{:S(2)}, u32[]{:S(2)}) collective-permute-start(bf16[2,128,128]{2,1,0:T(8,128)(2,1)S(1)} %get-tuple-element.38.gz), channel_id=1, source_target_pairs={{0,1},{1,2},{2,3},{3,4},{4,5},{5,6},{6,7},{7,8},{8,9},{9,10},{10,1... | collective-permute-start | bytes 196616 | tf_op jit(solution)/shard_map/ppermute | solution.py:351
  108.9 6.7 %collective-permute-start.20 = (bf16[2,64,128]{2,1,0:T(8,128)(2,1)S(1)}, bf16[2,64,128]{2,1,0:T(8,128)(2,1)S(1)}, u32[]{:S(2)}, u32[]{:S(2)}) collective-permute-start(bf16[2,64,128]{2,1,0:T(8,128)(2,1)S(1)} %get-tuple-element.39.low), channel_id=1, source_target_pairs={{64,0},{80,16},{96,32},{112,48},{128,64},{144,80},{160,96},{176,11... | collective-permute-start | bytes 98312 | tf_op jit(solution)/shard_map/ppermute | solution.py:360
  118.2 5.1 %collective-permute-start.22 = (bf16[2,128,128]{2,1,0:T(8,128)(2,1)S(1)}, bf16[2,128,128]{2,1,0:T(8,128)(2,1)S(1)}, u32[]{:S(2)}, u32[]{:S(2)}) collective-permute-start(bf16[2,128,128]{2,1,0:T(8,128)(2,1)S(1)} %get-tuple-element.43.gz), channel_id=1, source_target_pairs={{1,0},{2,1},{3,2},{4,3},{5,4},{6,5},{7,6},{8,7},{9,8},{10,9},{11,1... | collective-permute-start | bytes 196616 | tf_op jit(solution)/shard_map/ppermute | solution.py:351
  125.4 6.4 %collective-permute-start.24 = (bf16[2,64,128]{2,1,0:T(8,128)(2,1)S(1)}, bf16[2,64,128]{2,1,0:T(8,128)(2,1)S(1)}, u32[]{:S(2)}, u32[]{:S(2)}) collective-permute-start(bf16[2,64,128]{2,1,0:T(8,128)(2,1)S(1)} %get-tuple-element.44.low), channel_id=1, source_target_pairs={{32,0},{48,16},{64,32},{80,48},{96,64},{112,80},{128,96},{144,112}... | collective-permute-start | bytes 98312 | tf_op jit(solution)/shard_map/ppermute | solution.py:360
  131.9 5.8 %collective-permute-start.25 = (bf16[2,128,128]{2,1,0:T(8,128)(2,1)S(1)}, bf16[2,128,128]{2,1,0:T(8,128)(2,1)S(1)}, u32[]{:S(2)}, u32[]{:S(2)}) collective-permute-start(bf16[2,128,128]{2,1,0:T(8,128)(2,1)S(1)} %get-tuple-element.48.gz), channel_id=1, source_target_pairs={{0,1},{1,2},{2,3},{3,4},{4,5},{5,6},{6,7},{7,8},{8,9},{9,10},{10,1... | collective-permute-start | bytes 196616 | tf_op jit(solution)/shard_map/ppermute | solution.py:351
  135.0 5.1 %collective-permute-start.26 = (bf16[2,128,128]{2,1,0:T(8,128)(2,1)S(1)}, bf16[2,128,128]{2,1,0:T(8,128)(2,1)S(1)}, u32[]{:S(2)}, u32[]{:S(2)}) collective-permute-start(bf16[2,128,128]{2,1,0:T(8,128)(2,1)S(1)} %get-tuple-element.48.gz), channel_id=1, source_target_pairs={{1,0},{2,1},{3,2},{4,3},{5,4},{6,5},{7,6},{8,7},{9,8},{10,9},{11,1... | collective-permute-start | bytes 196616 | tf_op jit(solution)/shard_map/ppermute | solution.py:351
  140.9 18.8 %collective-permute-start.27 = (bf16[2,64,128]{2,1,0:T(8,128)(2,1)S(1)}, bf16[2,64,128]{2,1,0:T(8,128)(2,1)S(1)}, u32[]{:S(2)}, u32[]{:S(2)}) collective-permute-start(bf16[2,64,128]{2,1,0:T(8,128)(2,1)S(1)} %get-tuple-element.50.low), channel_id=1, source_target_pairs={{240,0},{0,16},{16,32},{32,48},{48,64},{64,80},{80,96},{96,112},{1... | collective-permute-start | bytes 98312 | tf_op jit(solution)/shard_map/ppermute | solution.py:360
  157.5 7.0 %collective-permute-start.28 = (bf16[2,64,128]{2,1,0:T(8,128)(2,1)S(1)}, bf16[2,64,128]{2,1,0:T(8,128)(2,1)S(1)}, u32[]{:S(2)}, u32[]{:S(2)}) collective-permute-start(bf16[2,64,128]{2,1,0:T(8,128)(2,1)S(1)} %get-tuple-element.50.low), channel_id=1, source_target_pairs={{16,0},{32,16},{48,32},{64,48},{80,64},{96,80},{112,96},{128,112},... | collective-permute-start | bytes 98312 | tf_op jit(solution)/shard_map/ppermute | solution.py:360
  169.5 23.5 %all-to-all-start.1 = ((bf16[8,512,128]{2,1,0:T(8,128)(2,1)}), bf16[8,512,128]{2,1,0:T(8,128)(2,1)S(1)}, u32[]{:S(2)}, u32[]{:S(2)}) async-start(bf16[8,512,128]{2,1,0:T(8,128)(2,1)} %shard_map.97), calls=%async_computation.1 | async-start | bytes 2097152 | tf_op jit(solution)/shard_map/all_to_all | solution.py:480
  175.7 14.4 %collective-permute-start.29 = (bf16[2,128,128]{2,1,0:T(8,128)(2,1)S(1)}, bf16[2,128,128]{2,1,0:T(8,128)(2,1)S(1)}, u32[]{:S(2)}, u32[]{:S(2)}) collective-permute-start(bf16[2,128,128]{2,1,0:T(8,128)(2,1)S(1)} %get-tuple-element.54.gz), channel_id=1, source_target_pairs={{0,1},{1,2},{2,3},{3,4},{4,5},{5,6},{6,7},{7,8},{8,9},{9,10},{10,1... | collective-permute-start | bytes 196616 | tf_op jit(solution)/shard_map/ppermute | solution.py:351
  180.2 11.8 %collective-permute-start.30 = (bf16[2,128,128]{2,1,0:T(8,128)(2,1)S(1)}, bf16[2,128,128]{2,1,0:T(8,128)(2,1)S(1)}, u32[]{:S(2)}, u32[]{:S(2)}) collective-permute-start(bf16[2,128,128]{2,1,0:T(8,128)(2,1)S(1)} %get-tuple-element.54.gz), channel_id=1, source_target_pairs={{1,0},{2,1},{3,2},{4,3},{5,4},{6,5},{7,6},{8,7},{9,8},{10,9},{11,1... | collective-permute-start | bytes 196616 | tf_op jit(solution)/shard_map/ppermute | solution.py:351
  209.4 20.3 %all-to-all-start.3 = ((bf16[16,48,128]{2,1,0:T(8,128)(2,1)}), bf16[16,48,128]{2,1,0:T(8,128)(2,1)S(1)}, u32[]{:S(2)}, u32[]{:S(2)}) async-start(bf16[16,48,128]{2,1,0:T(8,128)(2,1)} %shard_map.99), calls=%async_computation.3 | async-start | bytes 393216 | tf_op jit(solution)/shard_map/all_to_all | solution.py:507
  222.1 6.8 %collective-permute-start.32 = (bf16[1,64,128]{2,1,0:T(8,128)(2,1)S(1)}, bf16[1,64,128]{2,1,0:T(8,128)(2,1)S(1)}, u32[]{:S(2)}, u32[]{:S(2)}) collective-permute-start(bf16[1,64,128]{2,1,0:T(8,128)(2,1)S(1)} %get-tuple-element.76), channel_id=1, source_target_pairs={{16,0},{32,16},{48,32},{64,48},{80,64},{96,80},{112,96},{128,112},... | collective-permute-start | bytes 49160 | tf_op jit(solution)/shard_map/ppermute | solution.py:360
  (16 other events, 76.6 us)
